TPU v7x, 32 devices: a whole 2x2x4 slice. The times are simulated.
32 devices in a mesh: dp: 8 (over z, y), tensor: 4 (over x, core).
Axes of the slice: x: 2, y: 2, z: 4, core: 2. Of those that a mesh axis runs over, the one named last changes fastest.
Arguments:
- inputs: bfloat16 [16, 1024, 768], P('dp', 'tensor'), may hold values from -6 to 6
- random_blocks: int32 [12, 16, 3], P('tensor'), may hold values from 0 to 15
- query_weight: bfloat16 [768, 768], P('dp', 'tensor'), may hold values from -0.21875 to 0.21875
- query_bias: bfloat16 [768], P(('tensor', 'dp')), may hold values from -3 to 3
- key_weight: bfloat16 [768, 768], P('dp', 'tensor'), may hold values from -0.21875 to 0.21875
- value_weight: bfloat16 [768, 768], P('dp', 'tensor'), may hold values from -0.21875 to 0.21875
- value_bias: bfloat16 [768], P(('tensor', 'dp')), may hold values from -0.59765625 to 0.59765625
- out_weight: bfloat16 [768, 768], P('tensor', 'dp'), may hold values from -0.875 to 0.875
- out_bias: bfloat16 [768], P('dp'), may hold values from -3 to 3
- first_gain: bfloat16 [768], P('dp'), may hold values from 0.5 to 1.5
- first_shift: bfloat16 [768], P('dp'), may hold values from -3 to 3
- up_weight: bfloat16 [768, 3072], P('dp', 'tensor'), may hold values from -0.21875 to 0.21875
- up_bias: bfloat16 [3072], P(('tensor', 'dp')), may hold values from -3 to 3
- down_weight: bfloat16 [3072, 768], P('tensor', 'dp'), may hold values from -0.109375 to 0.109375
- down_bias: bfloat16 [768], P('dp'), may hold values from -3 to 3
- second_gain: bfloat16 [768], P('dp'), may hold values from 0.5 to 1.5
- second_shift: bfloat16 [768], P('dp'), may hold values from -3 to 3
- cotangent: bfloat16 [16, 1024, 768], P('dp', 'tensor'), may hold values from -6 to 6
Outputs:
- output: bfloat16 [16, 1024, 768], P('dp', 'tensor')
- input_grad: float32 [16, 1024, 768], P('dp', 'tensor')
- query_weight_grad: float32 [768, 768], P('dp', 'tensor')
- query_bias_grad: float32 [768], P(('tensor', 'dp'))
- key_weight_grad: float32 [768, 768], P('dp', 'tensor')
- value_weight_grad: float32 [768, 768], P('dp', 'tensor')
- value_bias_grad: float32 [768], P(('tensor', 'dp'))
- out_weight_grad: float32 [768, 768], P('tensor', 'dp')
- out_bias_grad: float32 [768], P('dp')
- first_gain_grad: float32 [768], P('dp')
- first_shift_grad: float32 [768], P('dp')
- up_weight_grad: float32 [768, 3072], P('dp', 'tensor')
- up_bias_grad: float32 [3072], P(('tensor', 'dp'))
- down_weight_grad: float32 [3072, 768], P('tensor', 'dp')
- down_bias_grad: float32 [768], P('dp')
- second_gain_grad: float32 [768], P('dp')
- second_shift_grad: float32 [768], P('dp')
Inputs may be any that keep to these rules, and one draw needn't show every extreme that they name: `random_blocks`: entry [h, i, r] names a key block of the same sequence that query block i attends to in head h; entries may repeat one another or fall on the window or the global blocks.
All inputs are finite; a program needn't handle non-finite values.
Results may differ from a plain program's by a relative error of at most 0.017.
Values may be sent and summed in bfloat16 or wider, within the bound.
A program may use at most 192 MiB of HBM per device.

v0:
```python
from functools import partial

import jax
import jax.numpy as jnp
from jax import lax
from jax.sharding import PartitionSpec as P

HEAD_DIM = 64
BLOCK = 64


norm_eps = 1e-12


def gather_weights(shards):
    return (
        lax.all_gather(shards[0], "dp", axis=0, tiled=True),
        lax.all_gather(shards[1], "dp", axis=0, tiled=True),
        lax.all_gather(shards[2], "dp", axis=0, tiled=True),
        lax.all_gather(shards[3], "dp", axis=0, tiled=True),
        lax.all_gather(shards[4], "dp", axis=0, tiled=True),
        lax.all_gather(shards[5], "dp", axis=1, tiled=True),
        lax.all_gather(shards[6], "dp", axis=0, tiled=True),
        lax.all_gather(shards[7], "dp", axis=0, tiled=True),
        lax.all_gather(shards[8], "dp", axis=0, tiled=True),
        lax.all_gather(shards[9], "dp", axis=0, tiled=True),
        lax.all_gather(shards[10], "dp", axis=0, tiled=True),
        lax.all_gather(shards[11], "dp", axis=1, tiled=True),
        lax.all_gather(shards[12], "dp", axis=0, tiled=True),
        lax.all_gather(shards[13], "dp", axis=0, tiled=True),
        lax.all_gather(shards[14], "dp", axis=0, tiled=True),
    )


def reduce_grads(grads):
    return (
        lax.psum_scatter(grads[0], "dp", scatter_dimension=0, tiled=True),
        lax.psum_scatter(grads[1], "dp", scatter_dimension=0, tiled=True),
        lax.psum_scatter(grads[2], "dp", scatter_dimension=0, tiled=True),
        lax.psum_scatter(grads[3], "dp", scatter_dimension=0, tiled=True),
        lax.psum_scatter(grads[4], "dp", scatter_dimension=0, tiled=True),
        lax.psum_scatter(grads[5], "dp", scatter_dimension=1, tiled=True),
        lax.psum_scatter(grads[6], "dp", scatter_dimension=0, tiled=True),
        lax.psum_scatter(grads[7], "dp", scatter_dimension=0, tiled=True),
        lax.psum_scatter(grads[8], "dp", scatter_dimension=0, tiled=True),
        lax.psum_scatter(grads[9], "dp", scatter_dimension=0, tiled=True),
        lax.psum_scatter(grads[10], "dp", scatter_dimension=0, tiled=True),
        lax.psum_scatter(grads[11], "dp", scatter_dimension=1, tiled=True),
        lax.psum_scatter(grads[12], "dp", scatter_dimension=0, tiled=True),
        lax.psum_scatter(grads[13], "dp", scatter_dimension=0, tiled=True),
        lax.psum_scatter(grads[14], "dp", scatter_dimension=0, tiled=True),
    )


def full_rows(block):
    return lax.all_gather(block, "tensor", axis=0, tiled=True)


def column_sums(partial_terms):
    return lax.psum_scatter(
        partial_terms.astype(jnp.bfloat16), "tensor", scatter_dimension=0, tiled=True
    ).astype(jnp.float32)


def block_allowed(random_blocks, block_count):
    row_ids = jnp.arange(block_count, dtype=jnp.int32)[:, None]
    col_ids = jnp.arange(block_count, dtype=jnp.int32)[None, :]
    fixed = (
        (jnp.abs(row_ids - col_ids) <= 1)
        | (col_ids == 0)
        | (col_ids == block_count - 1)
        | (row_ids == 0)
        | (row_ids == block_count - 1)
    )
    picked = jnp.any(
        random_blocks[:, :, :, None]
        == jnp.arange(block_count, dtype=jnp.int32)[None, None, None, :],
        axis=2,
    )
    return fixed[None, :, :] | picked


def layer_norm(values, gain, shift):
    mean = jnp.mean(values, axis=1, keepdims=True)
    spread = jnp.mean(values * values, axis=1, keepdims=True) - mean * mean
    factor = lax.rsqrt(spread + norm_eps)
    normed = (values - mean) * factor
    return (normed * gain + shift, normed, factor)


def norm_back(upstream, normed, factor, gain):
    scaled = upstream * gain
    plain = jnp.mean(scaled, axis=1, keepdims=True)
    along = jnp.mean(scaled * normed, axis=1, keepdims=True)
    back = factor * (scaled - plain - normed * along)
    return (back, jnp.sum(upstream * normed, axis=0), jnp.sum(upstream, axis=0))


def row_parts(array, span):
    return array.reshape((array.shape[0] // span, span) + array.shape[1:])


def mask_parts(allowed, span):
    return allowed.reshape(allowed.shape[0], -1, span // BLOCK, allowed.shape[2]).transpose(
        1, 0, 2, 3
    )


def block_scores(query_block, key_heads, mask_block):
    products = jnp.einsum(
        "qhd,khd->hqk", query_block, key_heads, preferred_element_type=jnp.float32
    )
    head_count, row_count, key_count = products.shape
    scaled = (products * HEAD_DIM ** (-0.5)).reshape(
        head_count, row_count // BLOCK, BLOCK, key_count // BLOCK, BLOCK
    )
    masked = jnp.where(mask_block[:, :, None, :, None], scaled, -1000000000.0)
    return masked.reshape(head_count, row_count, key_count)


def attend(query_heads, key_heads, value_heads, allowed):
    length = query_heads.shape[0]
    span = min(512, length)

    def one_part(items):
        query_block, mask_block = items
        scores = block_scores(query_block, key_heads, mask_block)
        largest = jnp.max(scores, axis=-1, keepdims=True)
        log_total = largest + jnp.log(jnp.sum(jnp.exp(scores - largest), axis=-1, keepdims=True))
        weights_low = jnp.exp(scores - log_total).astype(jnp.bfloat16)
        mixed = jnp.einsum(
            "hqk,khd->qhd", weights_low, value_heads, preferred_element_type=jnp.float32
        )
        return (mixed, log_total[..., 0])

    mixed, log_totals = lax.map(one_part, (row_parts(query_heads, span), mask_parts(allowed, span)))
    return (mixed.reshape(length, -1).astype(jnp.bfloat16), log_totals)


def attend_back(query_heads, key_heads, value_heads, mixed_back, log_totals, allowed):
    length = query_heads.shape[0]
    span = min(512, length)

    def one_part(carry, items):
        key_sum, value_sum = carry
        query_block, back_block, log_total, mask_block = items
        scores = block_scores(query_block, key_heads, mask_block)
        weights = jnp.exp(scores - log_total[..., None])
        weights_low = weights.astype(jnp.bfloat16)
        weights_back = jnp.einsum(
            "qhd,khd->hqk", back_block, value_heads, preferred_element_type=jnp.float32
        )
        centre = jnp.sum(weights_back * weights, axis=-1, keepdims=True)
        scores_back = (weights * (weights_back - centre) * HEAD_DIM ** (-0.5)).astype(jnp.bfloat16)
        query_back = jnp.einsum(
            "hqk,khd->qhd", scores_back, key_heads, preferred_element_type=jnp.float32
        )
        key_sum = key_sum + jnp.einsum(
            "hqk,qhd->khd", scores_back, query_block, preferred_element_type=jnp.float32
        )
        value_sum = value_sum + jnp.einsum(
            "hqk,qhd->khd", weights_low, back_block, preferred_element_type=jnp.float32
        )
        return ((key_sum, value_sum), query_back)

    empty = jnp.zeros(key_heads.shape, jnp.float32)
    (key_back, value_back), query_back = lax.scan(
        one_part,
        (empty, empty),
        (
            row_parts(query_heads, span),
            row_parts(mixed_back, span),
            log_totals,
            mask_parts(allowed, span),
        ),
    )
    return (
        query_back.reshape(length, -1).astype(jnp.bfloat16),
        key_back.reshape(length, -1).astype(jnp.bfloat16),
        value_back.reshape(length, -1).astype(jnp.bfloat16),
    )


def forward_pass(weights, token_block, allowed):
    (
        query_weight,
        query_bias,
        key_weight,
        value_weight,
        value_bias,
        out_weight,
        out_bias,
        first_gain,
        first_shift,
        up_weight,
        up_bias,
        down_weight,
        down_bias,
        second_gain,
        second_shift,
    ) = weights
    token_rows = full_rows(token_block)
    length = token_rows.shape[0]

    def heads_of(product):
        return product.astype(jnp.bfloat16).reshape(length, -1, HEAD_DIM)

    query_heads = heads_of(
        jnp.dot(token_rows, query_weight, preferred_element_type=jnp.float32) + query_bias
    )
    key_heads = heads_of(jnp.dot(token_rows, key_weight, preferred_element_type=jnp.float32))
    value_heads = heads_of(
        jnp.dot(token_rows, value_weight, preferred_element_type=jnp.float32) + value_bias
    )
    mixed, log_totals = attend(query_heads, key_heads, value_heads, allowed)
    branch_terms = jnp.dot(mixed, out_weight, preferred_element_type=jnp.float32)
    hidden = token_block.astype(jnp.float32) + column_sums(branch_terms) + out_bias
    first_norm, first_normed, first_factor = layer_norm(hidden, first_gain, first_shift)
    first_rows = full_rows(first_norm.astype(jnp.bfloat16))
    inner = jnp.dot(first_rows, up_weight, preferred_element_type=jnp.float32) + up_bias
    active = jax.nn.gelu(inner, approximate=False).astype(jnp.bfloat16)
    second_in = (
        first_norm
        + column_sums(jnp.dot(active, down_weight, preferred_element_type=jnp.float32))
        + down_bias
    )
    result, second_normed, second_factor = layer_norm(second_in, second_gain, second_shift)
    kept = (
        token_rows,
        query_heads,
        key_heads,
        value_heads,
        log_totals,
        mixed,
        first_normed,
        first_factor,
        first_rows,
        inner,
        active,
        second_normed,
        second_factor,
    )
    return (result, kept)


def backward_pass(weights, kept, upstream_block, allowed):
    (
        query_weight,
        query_bias,
        key_weight,
        value_weight,
        value_bias,
        out_weight,
        out_bias,
        first_gain,
        first_shift,
        up_weight,
        up_bias,
        down_weight,
        down_bias,
        second_gain,
        second_shift,
    ) = weights
    (
        token_rows,
        query_heads,
        key_heads,
        value_heads,
        log_totals,
        mixed,
        first_normed,
        first_factor,
        first_rows,
        inner,
        active,
        second_normed,
        second_factor,
    ) = kept
    length = token_rows.shape[0]
    upstream = upstream_block.astype(jnp.float32)
    second_back, second_gain_grad, second_shift_grad = norm_back(
        upstream, second_normed, second_factor, second_gain
    )
    down_bias_grad = jnp.sum(second_back, axis=0)
    feed_rows = full_rows(second_back.astype(jnp.bfloat16))
    down_weight_grad = jnp.einsum(
        "tf,td->fd", active, feed_rows, preferred_element_type=jnp.float32
    )
    active_back = jnp.einsum(
        "td,fd->tf", feed_rows, down_weight, preferred_element_type=jnp.float32
    )
    inner_back = jax.vjp(partial(jax.nn.gelu, approximate=False), inner)[1](active_back)[0].astype(
        jnp.bfloat16
    )
    up_bias_grad = jnp.sum(inner_back, axis=0, dtype=jnp.float32)
    up_weight_grad = jnp.einsum(
        "td,tf->df", first_rows, inner_back, preferred_element_type=jnp.float32
    )
    first_back = second_back + column_sums(
        jnp.einsum("tf,df->td", inner_back, up_weight, preferred_element_type=jnp.float32)
    )
    hidden_back, first_gain_grad, first_shift_grad = norm_back(
        first_back, first_normed, first_factor, first_gain
    )
    out_bias_grad = jnp.sum(hidden_back, axis=0)
    branch_rows = full_rows(hidden_back.astype(jnp.bfloat16))
    out_weight_grad = jnp.einsum(
        "tc,td->cd", mixed, branch_rows, preferred_element_type=jnp.float32
    )
    mixed_back = jnp.einsum(
        "td,cd->tc", branch_rows, out_weight, preferred_element_type=jnp.float32
    ).astype(jnp.bfloat16)
    query_back, key_back, value_back = attend_back(
        query_heads,
        key_heads,
        value_heads,
        mixed_back.reshape(length, -1, HEAD_DIM),
        log_totals,
        allowed,
    )
    query_weight_grad = jnp.einsum(
        "td,tc->dc", token_rows, query_back, preferred_element_type=jnp.float32
    )
    key_weight_grad = jnp.einsum(
        "td,tc->dc", token_rows, key_back, preferred_element_type=jnp.float32
    )
    value_weight_grad = jnp.einsum(
        "td,tc->dc", token_rows, value_back, preferred_element_type=jnp.float32
    )
    query_bias_grad = jnp.sum(query_back, axis=0, dtype=jnp.float32)
    value_bias_grad = jnp.sum(value_back, axis=0, dtype=jnp.float32)
    projected = (
        jnp.einsum("tc,dc->td", query_back, query_weight, preferred_element_type=jnp.float32)
        + jnp.einsum("tc,dc->td", key_back, key_weight, preferred_element_type=jnp.float32)
        + jnp.einsum("tc,dc->td", value_back, value_weight, preferred_element_type=jnp.float32)
    )
    input_back = hidden_back + column_sums(projected)
    grads = (
        query_weight_grad,
        query_bias_grad,
        key_weight_grad,
        value_weight_grad,
        value_bias_grad,
        out_weight_grad,
        out_bias_grad,
        first_gain_grad,
        first_shift_grad,
        up_weight_grad,
        up_bias_grad,
        down_weight_grad,
        down_bias_grad,
        second_gain_grad,
        second_shift_grad,
    )
    return (input_back, grads)


def local(
    inputs,
    random_blocks,
    query_weight,
    query_bias,
    key_weight,
    value_weight,
    value_bias,
    out_weight,
    out_bias,
    first_gain,
    first_shift,
    up_weight,
    up_bias,
    down_weight,
    down_bias,
    second_gain,
    second_shift,
    cotangent,
):
    shards = (
        query_weight,
        query_bias,
        key_weight,
        value_weight,
        value_bias,
        out_weight,
        out_bias,
        first_gain,
        first_shift,
        up_weight,
        up_bias,
        down_weight,
        down_bias,
        second_gain,
        second_shift,
    )
    allowed = block_allowed(random_blocks, random_blocks.shape[1])
    resident = gather_weights(shards)
    growth = lax.axis_size("dp")
    grown_dims = (0, 0, 0, 0, 0, 1, 0, 0, 0, 0, 0, 1, 0, 0, 0)
    start = tuple(
        (
            jnp.zeros(
                tuple(
                    (
                        extent * growth if position == grown_dim else extent
                        for position, extent in enumerate(shard.shape)
                    )
                ),
                jnp.float32,
            )
            for shard, grown_dim in zip(shards, grown_dims)
        )
    )

    def one_sequence(totals, items):
        token_block, upstream_block = items
        result, kept = forward_pass(resident, token_block, allowed)
        input_back, grads = backward_pass(resident, kept, upstream_block, allowed)
        totals = tuple((summed + update for summed, update in zip(totals, grads)))
        return (totals, (result.astype(jnp.bfloat16), input_back))

    totals, (results, input_backs) = lax.scan(one_sequence, start, (inputs, cotangent))
    shares = reduce_grads(totals)
    vectors = lax.psum(
        (shares[6], shares[7], shares[8], shares[12], shares[13], shares[14]), "tensor"
    )
    return (
        results,
        input_backs,
        shares[0],
        shares[1],
        shares[2],
        shares[3],
        shares[4],
        shares[5],
        vectors[0],
        vectors[1],
        vectors[2],
        shares[9],
        shares[10],
        shares[11],
        vectors[3],
        vectors[4],
        vectors[5],
    )


def solution(mesh):
    return jax.shard_map(
        local,
        mesh=mesh,
        in_specs=(
            P("dp", "tensor", None),
            P("tensor", None, None),
            P("dp", "tensor"),
            P(("tensor", "dp")),
            P("dp", "tensor"),
            P("dp", "tensor"),
            P(("tensor", "dp")),
            P("tensor", "dp"),
            P("dp"),
            P("dp"),
            P("dp"),
            P("dp", "tensor"),
            P(("tensor", "dp")),
            P("tensor", "dp"),
            P("dp"),
            P("dp"),
            P("dp"),
            P("dp", "tensor", None),
        ),
        out_specs=(
            P("dp", "tensor", None),
            P("dp", "tensor", None),
            P("dp", "tensor"),
            P(("tensor", "dp")),
            P("dp", "tensor"),
            P("dp", "tensor"),
            P(("tensor", "dp")),
            P("tensor", "dp"),
            P("dp"),
            P("dp"),
            P("dp"),
            P("dp", "tensor"),
            P(("tensor", "dp")),
            P("tensor", "dp"),
            P("dp"),
            P("dp"),
            P("dp"),
        ),
        check_vma=False,
    )
```

profile of v0, /device:TPU:0, one launch (start us, length us, event | category | flops | bytes accessed | tf_op | source)
XLA Modules:
  0.0 1385.6 jit_solution(12324565996378756680)
XLA Ops:
  12.4 33.5 %all_gather.62 = bf16[192,768]{0,1:T(8,128)(2,1)S(1)} all-gather(bf16[192,96]{0,1:T(8,128)(2,1)S(1)} %copy.79), channel_id=1, replica_groups=mesh['dp'=8,'tensor'=4] {'dp'}, dimensions={1}, use_global_device_ids=true | all-gather | bytes 331776 | tf_op jit(solution)/shard_map/all_gather | solution.py:22
  54.3 37.7 %all-reduce.20 = (bf16[192]{0:T(256)(128)(2,1)}, bf16[192]{0:T(256)(128)(2,1)}, bf16[768]{0:T(1024)(128)(2,1)}, bf16[768]{0:T(1024)(128)(2,1)}, bf16[768]{0:T(10...) all-reduce(bf16[192]{0:T(256)(128)(2,1)S(1)} %dynamic-update-slice,, ...), channel_id=1, replica_groups=mesh['dp'=8,'tensor'=4] {'dp'}, use_global_device_ids=true, to_apply=%add | all-reduce | flops 5760 | bytes 23040
  92.8 33.3 %all_gather.57 = bf16[768,192]{1,0:T(8,128)(2,1)} all-gather(bf16[96,192]{1,0:T(8,128)(2,1)} %param.26), channel_id=1, replica_groups=mesh['dp'=8,'tensor'=4] {'dp'}, dimensions={0}, use_global_device_ids=true | all-gather | bytes 331776 | tf_op jit(solution)/shard_map/all_gather | solution.py:17
  126.1 33.4 %all_gather.59 = bf16[768,192]{1,0:T(8,128)(2,1)} all-gather(bf16[96,192]{1,0:T(8,128)(2,1)} %param.28), channel_id=1, replica_groups=mesh['dp'=8,'tensor'=4] {'dp'}, dimensions={0}, use_global_device_ids=true | all-gather | bytes 331776 | tf_op jit(solution)/shard_map/all_gather | solution.py:19
  159.6 33.2 %all_gather.60 = bf16[768,192]{1,0:T(8,128)(2,1)} all-gather(bf16[96,192]{1,0:T(8,128)(2,1)} %param.29), channel_id=1, replica_groups=mesh['dp'=8,'tensor'=4] {'dp'}, dimensions={0}, use_global_device_ids=true | all-gather | bytes 331776 | tf_op jit(solution)/shard_map/all_gather | solution.py:20
  195.8 775.3 %while.74 = (s32[]{:T(128)}, f32[768,192]{0,1:T(8,128)}, f32[192]{0:T(256)}, f32[768,192]{0,1:T(8,128)}, f32[768,192]{0,1:T(8,128)}, /*index=5*/f32[192]{0:T(256...) while((s32[]{:T(128)}, f32[768,192]{0,1:T(8,128)}, ...), condition=%wide.region_30.31_spmd.clone, body=%wide.region_1.30_spmd.clone.sunk | while | flops 12414239744 | bytes 414117248 | solution.py:421
  222.1 16.3 %all-gather.15.cloned.1.call-done = bf16[1,1024,768]{2,1,0:T(8,128)(2,1)} async-done(((bf16[1,256,768]{2,1,0:T(8,128)(2,1)}), bf16[1,1024,768]{2,1,0:T(8,128)(2,1)}) %all-gather.15.cloned.1.call-update) | async-done | bytes 1572880 | tf_op jit(solution)/shard_map/while/body/eval_jaxpr/all_gather | solution.py:56
  245.2 35.6 %while.75 = (s32[]{:T(128)}, bf16[2,512,3,64]{1,3,2,0:T(8,128)(2,1)}, f32[2,3,512]{2,1,0:T(4,128)}, pred[2,3,8,16]{3,2,1,0:T(8,128)(4,1)S(1)}, bf16[2,512,3,64]{...) while((s32[]{:T(128)}, ...), condition=%wide.region_5.5_spmd, body=%wide.region_2.4_spmd.sunk | while | flops 419953152 | bytes 32888100 | solution.py:136
  247.7 8.5 broadcast_in_dim.115
  265.5 8.5 broadcast_in_dim.115
  286.0 28.2 %reduce-scatter.25.cloned.1.call-done = bf16[256,768]{1,0:T(8,128)(2,1)} async-done(((bf16[1024,768]{1,0:T(8,128)(2,1)}), bf16[256,768]{1,0:T(8,128)(2,1)}) %reduce-scatter.25.cloned.1.call-update) | async-done | bytes 393232 | tf_op jit(solution)/shard_map/while/body/eval_jaxpr/reduce_scatter | solution.py:60
  317.6 19.7 %all-gather.17.cloned.1.call-done = bf16[1024,768]{1,0:T(8,128)(2,1)} async-done(((bf16[256,768]{1,0:T(8,128)(2,1)}), bf16[1024,768]{1,0:T(8,128)(2,1)}) %all-gather.17.cloned.1.call-update) | async-done | bytes 1572880 | tf_op jit(solution)/shard_map/while/body/eval_jaxpr/all_gather | solution.py:56
  337.3 10.9 multiply_convert_fusion.3
  352.2 28.2 %reduce-scatter.27.cloned.1.call-done = bf16[256,768]{1,0:T(8,128)(2,1)} async-done(((bf16[1024,768]{1,0:T(8,128)(2,1)}), bf16[256,768]{1,0:T(8,128)(2,1)}) %reduce-scatter.27.cloned.1.call-update) | async-done | bytes 393232 | tf_op jit(solution)/shard_map/while/body/eval_jaxpr/reduce_scatter | solution.py:60
  384.7 19.8 %all-gather.19.cloned.1.call-done = bf16[1024,768]{1,0:T(8,128)(2,1)} async-done(((bf16[256,768]{1,0:T(8,128)(2,1)}), bf16[1024,768]{1,0:T(8,128)(2,1)}) %all-gather.19.cloned.1.call-update) | async-done | bytes 1572880 | tf_op jit(solution)/shard_map/while/body/eval_jaxpr/all_gather | solution.py:56
  404.5 6.5 convert_reduce_fusion.8
  414.9 28.3 %reduce-scatter.29.cloned.1.call-done = bf16[256,768]{1,0:T(8,128)(2,1)} async-done(((bf16[1024,768]{1,0:T(8,128)(2,1)}), bf16[256,768]{1,0:T(8,128)(2,1)}) %reduce-scatter.29.cloned.1.call-update) | async-done | bytes 393232 | tf_op jit(solution)/shard_map/while/body/eval_jaxpr/reduce_scatter | solution.py:60
  450.9 17.6 %all-gather.21.cloned.1.call-done = bf16[1024,768]{1,0:T(8,128)(2,1)} async-done(((bf16[256,768]{1,0:T(8,128)(2,1)}), bf16[1024,768]{1,0:T(8,128)(2,1)}) %all-gather.21.cloned.1.call-update) | async-done | bytes 1572880 | tf_op jit(solution)/shard_map/while/body/eval_jaxpr/all_gather | solution.py:56
  472.5 81.6 %while.76 = (s32[]{:T(128)}, f32[1024,3,64]{0,2,1:T(8,128)}, f32[1024,3,64]{0,2,1:T(8,128)}, bf16[2,512,3,64]{1,3,2,0:T(8,128)(2,1)}, bf16[2,512,3,64]{1,3,2,0:T...) while((s32[]{:T(128)}, f32[1024,3,64]{0,2,1:T(8,128)}, ...), condition=%wide.region_19.19_spmd.clone, body=%wide.region_17.18_spmd.clone.sunk | while | flops 1029444608 | bytes 129781360 | solution.py:167
  474.9 7.8 broadcast_in_dim.118
  482.7 3.4 subtract_exponential_fusion.2
  488.8 3.7 fusion.293
  492.6 9.9 fusion.296
  502.5 9.9 fusion.294
  515.8 7.8 broadcast_in_dim.118
  523.5 3.4 subtract_exponential_fusion.2
  529.7 3.7 fusion.293
  533.4 9.9 fusion.296
  543.3 9.9 fusion.294
  562.3 4.4 select_add_fusion.24
  576.8 13.8 reduce-scatter.31.cloned.1.call-done
  595.4 19.2 %all-gather.15.cloned.1.call-done = bf16[1,1024,768]{2,1,0:T(8,128)(2,1)} async-done(((bf16[1,256,768]{2,1,0:T(8,128)(2,1)}), bf16[1,1024,768]{2,1,0:T(8,128)(2,1)}) %all-gather.15.cloned.1.call-update) | async-done | bytes 1572880 | tf_op jit(solution)/shard_map/while/body/eval_jaxpr/all_gather | solution.py:56
  621.3 35.6 %while.75 = (s32[]{:T(128)}, bf16[2,512,3,64]{1,3,2,0:T(8,128)(2,1)}, f32[2,3,512]{2,1,0:T(4,128)}, pred[2,3,8,16]{3,2,1,0:T(8,128)(4,1)S(1)}, bf16[2,512,3,64]{...) while((s32[]{:T(128)}, ...), condition=%wide.region_5.5_spmd, body=%wide.region_2.4_spmd.sunk | while | flops 419953152 | bytes 32888100 | solution.py:136
  623.9 8.5 broadcast_in_dim.115
  641.7 8.5 broadcast_in_dim.115
  662.1 28.2 %reduce-scatter.25.cloned.1.call-done = bf16[256,768]{1,0:T(8,128)(2,1)} async-done(((bf16[1024,768]{1,0:T(8,128)(2,1)}), bf16[256,768]{1,0:T(8,128)(2,1)}) %reduce-scatter.25.cloned.1.call-update) | async-done | bytes 393232 | tf_op jit(solution)/shard_map/while/body/eval_jaxpr/reduce_scatter | solution.py:60
  693.7 19.7 %all-gather.17.cloned.1.call-done = bf16[1024,768]{1,0:T(8,128)(2,1)} async-done(((bf16[256,768]{1,0:T(8,128)(2,1)}), bf16[1024,768]{1,0:T(8,128)(2,1)}) %all-gather.17.cloned.1.call-update) | async-done | bytes 1572880 | tf_op jit(solution)/shard_map/while/body/eval_jaxpr/all_gather | solution.py:56
  713.5 10.9 multiply_convert_fusion.3
  728.4 28.2 %reduce-scatter.27.cloned.1.call-done = bf16[256,768]{1,0:T(8,128)(2,1)} async-done(((bf16[1024,768]{1,0:T(8,128)(2,1)}), bf16[256,768]{1,0:T(8,128)(2,1)}) %reduce-scatter.27.cloned.1.call-update) | async-done | bytes 393232 | tf_op jit(solution)/shard_map/while/body/eval_jaxpr/reduce_scatter | solution.py:60
  760.8 19.8 %all-gather.19.cloned.1.call-done = bf16[1024,768]{1,0:T(8,128)(2,1)} async-done(((bf16[256,768]{1,0:T(8,128)(2,1)}), bf16[1024,768]{1,0:T(8,128)(2,1)}) %all-gather.19.cloned.1.call-update) | async-done | bytes 1572880 | tf_op jit(solution)/shard_map/while/body/eval_jaxpr/all_gather | solution.py:56
  780.6 6.5 convert_reduce_fusion.8
  791.0 28.3 %reduce-scatter.29.cloned.1.call-done = bf16[256,768]{1,0:T(8,128)(2,1)} async-done(((bf16[1024,768]{1,0:T(8,128)(2,1)}), bf16[256,768]{1,0:T(8,128)(2,1)}) %reduce-scatter.29.cloned.1.call-update) | async-done | bytes 393232 | tf_op jit(solution)/shard_map/while/body/eval_jaxpr/reduce_scatter | solution.py:60
  827.0 17.6 %all-gather.21.cloned.1.call-done = bf16[1024,768]{1,0:T(8,128)(2,1)} async-done(((bf16[256,768]{1,0:T(8,128)(2,1)}), bf16[1024,768]{1,0:T(8,128)(2,1)}) %all-gather.21.cloned.1.call-update) | async-done | bytes 1572880 | tf_op jit(solution)/shard_map/while/body/eval_jaxpr/all_gather | solution.py:56
  848.6 81.6 %while.76 = (s32[]{:T(128)}, f32[1024,3,64]{0,2,1:T(8,128)}, f32[1024,3,64]{0,2,1:T(8,128)}, bf16[2,512,3,64]{1,3,2,0:T(8,128)(2,1)}, bf16[2,512,3,64]{1,3,2,0:T...) while((s32[]{:T(128)}, f32[1024,3,64]{0,2,1:T(8,128)}, ...), condition=%wide.region_19.19_spmd.clone, body=%wide.region_17.18_spmd.clone.sunk | while | flops 1029444608 | bytes 129781360 | solution.py:167
  851.1 7.8 broadcast_in_dim.118
  865.0 3.7 fusion.293
  868.7 9.9 fusion.296
  878.6 9.9 fusion.294
  891.9 7.8 broadcast_in_dim.118
  899.7 3.4 subtract_exponential_fusion.2
  905.8 3.7 fusion.293
  909.5 9.9 fusion.296
  919.4 9.9 fusion.294
  938.4 5.1 select_add_fusion.24
  943.7 4.6 select_add_fusion.22
  956.4 10.3 reduce-scatter.31.cloned.1.call-done
  983.8 37.2 %all-reduce.18 = (f32[192]{0:T(256)S(1)}, f32[192]{0:T(256)S(1)}, f32[768]{0:T(1024)S(1)}, f32[768]{0:T(1024)S(1)}, f32[768]{0:T(1024)S(1)}, /*index=5*/f32[768]...) all-reduce(f32[192]{0:T(256)S(1)} %copy-done.81, ...), channel_id=8, replica_groups=mesh['dp'=8,'tensor'=4] {'dp'}, use_global_device_ids=true, to_apply=%region_32.33.clone | all-reduce | flops 5760 | bytes 46080
  1023.2 6.4 all-reduce.19
  1029.5 8.3 reduce-scatter.23.cloned.1.call-done
  1039.5 64.0 %reduce-scatter.13.cloned.1.call-done = f32[96,192]{1,0:T(8,128)} async-done(((f32[768,192]{1,0:T(8,128)}), f32[96,192]{1,0:T(8,128)}) %reduce-scatter.13.cloned.1.call-update) | async-done | bytes 73744 | tf_op jit(solution)/shard_map/reduce_scatter | solution.py:37
  1103.5 65.3 %reduce-scatter.15.cloned.1.call-done = f32[96,192]{1,0:T(8,128)} async-done(((f32[768,192]{1,0:T(8,128)}), f32[96,192]{1,0:T(8,128)}) %reduce-scatter.15.cloned.1.call-update) | async-done | bytes 73744 | tf_op jit(solution)/shard_map/reduce_scatter | solution.py:39
  1168.7 65.9 %reduce-scatter.17.cloned.1.call-done = f32[96,192]{1,0:T(8,128)} async-done(((f32[768,192]{1,0:T(8,128)}), f32[96,192]{1,0:T(8,128)}) %reduce-scatter.17.cloned.1.call-update) | async-done | bytes 73744 | tf_op jit(solution)/shard_map/reduce_scatter | solution.py:40
  1234.6 72.0 %reduce-scatter.19.cloned.1.call-done = f32[96,768]{1,0:T(8,128)} async-done(((f32[768,768]{1,0:T(8,128)}), f32[96,768]{1,0:T(8,128)}) %reduce-scatter.19.cloned.1.call-update) | async-done | bytes 294928 | tf_op jit(solution)/shard_map/reduce_scatter | solution.py:46
  1306.6 72.0 %reduce-scatter.21.cloned.1.call-done = f32[768,96]{0,1:T(8,128)} async-done(((f32[768,768]{0,1:T(8,128)}), f32[768,96]{0,1:T(8,128)}) %reduce-scatter.21.cloned.1.call-update) | async-done | bytes 294928 | tf_op jit(solution)/shard_map/reduce_scatter | solution.py:48
  (666 shorter events, 216.4 us)
Async XLA Ops:
  7.2 188.6 %copy-start.12 = (bf16[2,256,768]{2,1,0:T(8,128)(2,1)S(1)}, bf16[2,256,768]{2,1,0:T(8,128)(2,1)}, u32[]{:S(2)}) copy-start(bf16[2,256,768]{2,1,0:T(8,128)(2,1)} %param.24) | copy-start | bytes 2359300
  7.2 186.2 %all-gather.13.cloned.1.call-start = ((), (), s32[]{:S(2)}) async-start(), calls=%async_computation.11 | async-start | bytes 1327104 | tf_op jit(solution)/shard_map/all_gather | solution.py:28
  7.9 187.9 %all-gather.11.cloned.1.call-start = ((), (), s32[]{:S(2)}) async-start(), calls=%async_computation.10 | async-start | bytes 1327104 | tf_op jit(solution)/shard_map/all_gather | solution.py:26
  219.2 19.3 %all-gather.15.cloned.1.call-start = ((), (), s32[]{:S(2)}) async-start(), calls=%async_computation.18 | async-start | bytes 1966080 | tf_op jit(solution)/shard_map/while/body/eval_jaxpr/all_gather | solution.py:56
  220.1 94.1 %reduce-scatter.25.cloned.1.call-start = ((), (), s32[]{:S(2)}) async-start(), calls=%async_computation.19 | async-start | bytes 1966080 | tf_op jit(solution)/shard_map/while/body/eval_jaxpr/reduce_scatter | solution.py:60
  282.3 35.2 %copy-start.72 = (bf16[768]{0:T(1024)(128)(2,1)S(1)}, bf16[768]{0:T(1024)(128)(2,1)}, u32[]{:S(2)}) copy-start(bf16[768]{0:T(1024)(128)(2,1)} %get-tuple-element.1412) | copy-start | bytes 4612 | tf_op jit(solution)/shard_map/while
  285.9 51.5 %all-gather.17.cloned.1.call-start = ((), (), s32[]{:S(2)}) async-start(), calls=%async_computation.20 | async-start | bytes 1966080 | tf_op jit(solution)/shard_map/while/body/eval_jaxpr/all_gather | solution.py:56
  286.0 62.3 %copy-start.36 = (f32[768]{0:T(1024)}, f32[768]{0:T(1024)S(1)}, u32[]{:S(2)}) copy-start(f32[768]{0:T(1024)S(1)} %convert_element_type.385) | copy-start | bytes 9220 | tf_op jit(solution)/shard_map/while
  315.5 32.8 %copy-start.37 = (f32[256]{0:T(256)}, f32[256]{0:T(256)S(1)}, u32[]{:S(2)}) copy-start(f32[256]{0:T(256)S(1)} %get-tuple-element.1182) | copy-start | bytes 3076 | tf_op jit(solution)/shard_map/while
  315.5 32.8 %copy-start.39 = (f32[256]{0:T(256)}, f32[256]{0:T(256)S(1)}, u32[]{:S(2)}) copy-start(f32[256]{0:T(256)S(1)} %get-tuple-element.1181) | copy-start | bytes 3076 | tf_op jit(solution)/shard_map/while
  317.5 63.0 %reduce-scatter.27.cloned.1.call-start = ((), (), s32[]{:S(2)}) async-start(), calls=%async_computation.21 | async-start | bytes 1966080 | tf_op jit(solution)/shard_map/while/body/eval_jaxpr/reduce_scatter | solution.py:60
  317.6 30.7 %copy-start.67 = (f32[768]{0:T(1024)}, f32[768]{0:T(1024)S(1)}, u32[]{:S(2)}) copy-start(f32[768]{0:T(1024)S(1)} %convert_element_type.384) | copy-start | bytes 9220 | tf_op jit(solution)/shard_map/while
  337.3 12.2 copy-start.35
  349.5 31.0 %copy-start.11 = (bf16[256,768]{1,0:T(8,128)(2,1)S(1)}, bf16[256,768]{1,0:T(8,128)(2,1)}, u32[]{:S(2)}) copy-start(bf16[256,768]{1,0:T(8,128)(2,1)} %reduce-scatter.25.cloned.1.call-done) | copy-start | bytes 1179652 | tf_op jit(solution)/shard_map/while
  352.1 30.0 %copy-start.23 = (bf16[2,256,768]{2,1,0:T(8,128)(2,1)S(1)}, bf16[2,256,768]{2,1,0:T(8,128)(2,1)}, u32[]{:S(2)}) copy-start(bf16[2,256,768]{2,1,0:T(8,128)(2,1)} %get-tuple-element.1415) | copy-start | bytes 2359300 | tf_op jit(solution)/shard_map/while
  352.1 52.4 %copy-start.68 = (f32[768]{0:T(1024)S(1)}, f32[768]{0:T(1024)}, u32[]{:S(2)}) copy-start(f32[768]{0:T(1024)} %copy-done.67) | copy-start | bytes 9220 | tf_op jit(solution)/shard_map/while
  352.1 52.3 %all-gather.19.cloned.1.call-start = ((), (), s32[]{:S(2)}) async-start(), calls=%async_computation.22 | async-start | bytes 1966080 | tf_op jit(solution)/shard_map/while/body/eval_jaxpr/all_gather | solution.py:56
  384.7 58.5 %copy-start.16 = (f32[256,768]{1,0:T(8,128)}, f32[256,768]{1,0:T(8,128)S(1)}, u32[]{:S(2)}) copy-start(f32[256,768]{1,0:T(8,128)S(1)} %get-tuple-element.1191) | copy-start | bytes 2359300 | tf_op jit(solution)/shard_map/while
  384.7 58.5 %reduce-scatter.29.cloned.1.call-start = ((), (), s32[]{:S(2)}) async-start(), calls=%async_computation.23 | async-start | bytes 1966080 | tf_op jit(solution)/shard_map/while/body/eval_jaxpr/reduce_scatter | solution.py:60
  412.2 30.9 %copy-start.38 = (f32[256]{0:T(256)S(1)}, f32[256]{0:T(256)}, u32[]{:S(2)}) copy-start(f32[256]{0:T(256)} %copy-done.37) | copy-start | bytes 3076 | tf_op jit(solution)/shard_map/while
  412.2 30.9 %copy-start.40 = (f32[256]{0:T(256)S(1)}, f32[256]{0:T(256)}, u32[]{:S(2)}) copy-start(f32[256]{0:T(256)} %copy-done.39) | copy-start | bytes 3076 | tf_op jit(solution)/shard_map/while
  414.8 53.7 %all-gather.21.cloned.1.call-start = ((), (), s32[]{:S(2)}) async-start(), calls=%async_computation.24 | async-start | bytes 1966080 | tf_op jit(solution)/shard_map/while/body/eval_jaxpr/all_gather | solution.py:56
  445.5 23.1 %copy-start.33 = (bf16[192,768]{1,0:T(8,128)(2,1)S(1)}, bf16[192,768]{1,0:T(8,128)(2,1)}, u32[]{:S(2)}) copy-start(bf16[192,768]{1,0:T(8,128)(2,1)} %get-tuple-element.1407) | copy-start | bytes 884740 | tf_op jit(solution)/shard_map/while
  447.8 23.9 %copy-start.14 = (f32[256,768]{1,0:T(8,128)}, f32[256,768]{1,0:T(8,128)S(1)}, u32[]{:S(2)}) copy-start(f32[256,768]{1,0:T(8,128)S(1)} %get-tuple-element.1198) | copy-start | bytes 2359300 | tf_op jit(solution)/shard_map/while
  448.7 141.8 %reduce-scatter.31.cloned.1.call-start = ((), (), s32[]{:S(2)}) async-start(), calls=%async_computation.25 | async-start | bytes 1966080 | tf_op jit(solution)/shard_map/while/body/eval_jaxpr/reduce_scatter | solution.py:60
  449.9 22.6 %copy-start.46 = (f32[768]{0:T(1024)}, f32[768]{0:T(1024)S(1)}, u32[]{:S(2)}) copy-start(f32[768]{0:T(1024)S(1)} %select_add_fusion.26) | copy-start | bytes 9220 | tf_op jit(solution)/shard_map/while
  450.0 22.5 %copy-start.49 = (f32[768]{0:T(1024)}, f32[768]{0:T(1024)S(1)}, u32[]{:S(2)}) copy-start(f32[768]{0:T(1024)S(1)} %select_add_fusion.25) | copy-start | bytes 9220 | tf_op jit(solution)/shard_map/while
  502.5 9.9 copy-start.18
  543.3 9.9 copy-start.18
  573.8 16.7 %copy-start.15 = (f32[256,768]{1,0:T(8,128)S(1)}, f32[256,768]{1,0:T(8,128)}, u32[]{:S(2)}) copy-start(f32[256,768]{1,0:T(8,128)} %copy-done.14) | copy-start | bytes 2359300 | tf_op jit(solution)/shard_map/while
  574.6 17.9 %copy-start.13 = (bf16[2,256,768]{2,1,0:T(8,128)(2,1)S(1)}, bf16[2,256,768]{2,1,0:T(8,128)(2,1)}, u32[]{:S(2)}) copy-start(bf16[2,256,768]{2,1,0:T(8,128)(2,1)} %get-tuple-element.1487) | copy-start | bytes 2359300 | tf_op jit(solution)/shard_map/while
  592.5 22.1 %all-gather.15.cloned.1.call-start = ((), (), s32[]{:S(2)}) async-start(), calls=%async_computation.18 | async-start | bytes 1966080 | tf_op jit(solution)/shard_map/while/body/eval_jaxpr/all_gather | solution.py:56
  593.3 97.0 %reduce-scatter.25.cloned.1.call-start = ((), (), s32[]{:S(2)}) async-start(), calls=%async_computation.19 | async-start | bytes 1966080 | tf_op jit(solution)/shard_map/while/body/eval_jaxpr/reduce_scatter | solution.py:60
  658.5 35.2 %copy-start.72 = (bf16[768]{0:T(1024)(128)(2,1)S(1)}, bf16[768]{0:T(1024)(128)(2,1)}, u32[]{:S(2)}) copy-start(bf16[768]{0:T(1024)(128)(2,1)} %get-tuple-element.1412) | copy-start | bytes 4612 | tf_op jit(solution)/shard_map/while
  662.0 51.5 %all-gather.17.cloned.1.call-start = ((), (), s32[]{:S(2)}) async-start(), calls=%async_computation.20 | async-start | bytes 1966080 | tf_op jit(solution)/shard_map/while/body/eval_jaxpr/all_gather | solution.py:56
  662.1 62.3 %copy-start.36 = (f32[768]{0:T(1024)}, f32[768]{0:T(1024)S(1)}, u32[]{:S(2)}) copy-start(f32[768]{0:T(1024)S(1)} %convert_element_type.385) | copy-start | bytes 9220 | tf_op jit(solution)/shard_map/while
  691.6 32.8 %copy-start.37 = (f32[256]{0:T(256)}, f32[256]{0:T(256)S(1)}, u32[]{:S(2)}) copy-start(f32[256]{0:T(256)S(1)} %get-tuple-element.1182) | copy-start | bytes 3076 | tf_op jit(solution)/shard_map/while
  691.6 32.8 %copy-start.39 = (f32[256]{0:T(256)}, f32[256]{0:T(256)S(1)}, u32[]{:S(2)}) copy-start(f32[256]{0:T(256)S(1)} %get-tuple-element.1181) | copy-start | bytes 3076 | tf_op jit(solution)/shard_map/while
  693.6 63.0 %reduce-scatter.27.cloned.1.call-start = ((), (), s32[]{:S(2)}) async-start(), calls=%async_computation.21 | async-start | bytes 1966080 | tf_op jit(solution)/shard_map/while/body/eval_jaxpr/reduce_scatter | solution.py:60
  693.7 30.7 %copy-start.67 = (f32[768]{0:T(1024)}, f32[768]{0:T(1024)S(1)}, u32[]{:S(2)}) copy-start(f32[768]{0:T(1024)S(1)} %convert_element_type.384) | copy-start | bytes 9220 | tf_op jit(solution)/shard_map/while
  713.5 12.2 copy-start.35
  725.6 31.0 %copy-start.11 = (bf16[256,768]{1,0:T(8,128)(2,1)S(1)}, bf16[256,768]{1,0:T(8,128)(2,1)}, u32[]{:S(2)}) copy-start(bf16[256,768]{1,0:T(8,128)(2,1)} %reduce-scatter.25.cloned.1.call-done) | copy-start | bytes 1179652 | tf_op jit(solution)/shard_map/while
  728.2 30.0 %copy-start.23 = (bf16[2,256,768]{2,1,0:T(8,128)(2,1)S(1)}, bf16[2,256,768]{2,1,0:T(8,128)(2,1)}, u32[]{:S(2)}) copy-start(bf16[2,256,768]{2,1,0:T(8,128)(2,1)} %get-tuple-element.1415) | copy-start | bytes 2359300 | tf_op jit(solution)/shard_map/while
  728.3 52.3 %copy-start.68 = (f32[768]{0:T(1024)S(1)}, f32[768]{0:T(1024)}, u32[]{:S(2)}) copy-start(f32[768]{0:T(1024)} %copy-done.67) | copy-start | bytes 9220 | tf_op jit(solution)/shard_map/while
  728.3 52.3 %all-gather.19.cloned.1.call-start = ((), (), s32[]{:S(2)}) async-start(), calls=%async_computation.22 | async-start | bytes 1966080 | tf_op jit(solution)/shard_map/while/body/eval_jaxpr/all_gather | solution.py:56
  760.8 58.5 %copy-start.16 = (f32[256,768]{1,0:T(8,128)}, f32[256,768]{1,0:T(8,128)S(1)}, u32[]{:S(2)}) copy-start(f32[256,768]{1,0:T(8,128)S(1)} %get-tuple-element.1191) | copy-start | bytes 2359300 | tf_op jit(solution)/shard_map/while
  760.8 58.5 %reduce-scatter.29.cloned.1.call-start = ((), (), s32[]{:S(2)}) async-start(), calls=%async_computation.23 | async-start | bytes 1966080 | tf_op jit(solution)/shard_map/while/body/eval_jaxpr/reduce_scatter | solution.py:60
  788.4 30.9 %copy-start.38 = (f32[256]{0:T(256)S(1)}, f32[256]{0:T(256)}, u32[]{:S(2)}) copy-start(f32[256]{0:T(256)} %copy-done.37) | copy-start | bytes 3076 | tf_op jit(solution)/shard_map/while
  788.4 30.9 %copy-start.40 = (f32[256]{0:T(256)S(1)}, f32[256]{0:T(256)}, u32[]{:S(2)}) copy-start(f32[256]{0:T(256)} %copy-done.39) | copy-start | bytes 3076 | tf_op jit(solution)/shard_map/while
  791.0 53.7 %all-gather.21.cloned.1.call-start = ((), (), s32[]{:S(2)}) async-start(), calls=%async_computation.24 | async-start | bytes 1966080 | tf_op jit(solution)/shard_map/while/body/eval_jaxpr/all_gather | solution.py:56
  821.6 23.1 %copy-start.33 = (bf16[192,768]{1,0:T(8,128)(2,1)S(1)}, bf16[192,768]{1,0:T(8,128)(2,1)}, u32[]{:S(2)}) copy-start(bf16[192,768]{1,0:T(8,128)(2,1)} %get-tuple-element.1407) | copy-start | bytes 884740 | tf_op jit(solution)/shard_map/while
  824.0 23.9 %copy-start.14 = (f32[256,768]{1,0:T(8,128)}, f32[256,768]{1,0:T(8,128)S(1)}, u32[]{:S(2)}) copy-start(f32[256,768]{1,0:T(8,128)S(1)} %get-tuple-element.1198) | copy-start | bytes 2359300 | tf_op jit(solution)/shard_map/while
  824.9 141.8 %reduce-scatter.31.cloned.1.call-start = ((), (), s32[]{:S(2)}) async-start(), calls=%async_computation.25 | async-start | bytes 1966080 | tf_op jit(solution)/shard_map/while/body/eval_jaxpr/reduce_scatter | solution.py:60
  826.1 22.6 %copy-start.46 = (f32[768]{0:T(1024)}, f32[768]{0:T(1024)S(1)}, u32[]{:S(2)}) copy-start(f32[768]{0:T(1024)S(1)} %select_add_fusion.26) | copy-start | bytes 9220 | tf_op jit(solution)/shard_map/while
  826.1 22.5 %copy-start.49 = (f32[768]{0:T(1024)}, f32[768]{0:T(1024)S(1)}, u32[]{:S(2)}) copy-start(f32[768]{0:T(1024)S(1)} %select_add_fusion.25) | copy-start | bytes 9220 | tf_op jit(solution)/shard_map/while
  878.6 9.9 copy-start.18
  952.4 14.3 %copy-start.15 = (f32[256,768]{1,0:T(8,128)S(1)}, f32[256,768]{1,0:T(8,128)}, u32[]{:S(2)}) copy-start(f32[256,768]{1,0:T(8,128)} %copy-done.14) | copy-start | bytes 2359300 | tf_op jit(solution)/shard_map/while
  953.2 15.4 %copy-start.13 = (bf16[2,256,768]{2,1,0:T(8,128)(2,1)S(1)}, bf16[2,256,768]{2,1,0:T(8,128)(2,1)}, u32[]{:S(2)}) copy-start(bf16[2,256,768]{2,1,0:T(8,128)(2,1)} %get-tuple-element.1487) | copy-start | bytes 2359300 | tf_op jit(solution)/shard_map/while
  971.1 66.7 %reduce-scatter.23.cloned.1.call-start = ((), (), s32[]{:S(2)}) async-start(), calls=%async_computation.17 | async-start | bytes 884736
  973.5 130.0 %reduce-scatter.13.cloned.1.call-start = ((), (), s32[]{:S(2)}) async-start(), calls=%async_computation.12 | async-start | bytes 884736 | tf_op jit(solution)/shard_map/reduce_scatter | solution.py:37
  975.8 192.9 %reduce-scatter.15.cloned.1.call-start = ((), (), s32[]{:S(2)}) async-start(), calls=%async_computation.13 | async-start | bytes 884736 | tf_op jit(solution)/shard_map/reduce_scatter | solution.py:39
  978.3 256.3 %reduce-scatter.17.cloned.1.call-start = ((), (), s32[]{:S(2)}) async-start(), calls=%async_computation.14 | async-start | bytes 884736 | tf_op jit(solution)/shard_map/reduce_scatter | solution.py:40
  979.5 327.0 %reduce-scatter.19.cloned.1.call-start = ((), (), s32[]{:S(2)}) async-start(), calls=%async_computation.15 | async-start | bytes 2654208 | tf_op jit(solution)/shard_map/reduce_scatter | solution.py:46
  980.3 398.3 %reduce-scatter.21.cloned.1.call-start = ((), (), s32[]{:S(2)}) async-start(), calls=%async_computation.16 | async-start | bytes 2654208 | tf_op jit(solution)/shard_map/reduce_scatter | solution.py:48
  (152 other events, 557.2 us)
Sparse Core Ops, SparseCore 0:
  10.2 44.7 all-gather.12
  57.2 40.0 all-gather.10
  221.6 16.8 all-gather.14
  286.0 28.1 reduce-scatter.24
  317.6 19.6 all-gather.16
  352.3 28.1 reduce-scatter.26
  384.8 19.6 all-gather.18
  415.0 28.1 reduce-scatter.28
  448.9 19.6 all-gather.20
  562.3 28.1 reduce-scatter.30
  594.9 19.6 all-gather.14
  662.1 28.1 reduce-scatter.24
  693.8 19.6 all-gather.16
  728.4 28.1 reduce-scatter.26
  760.9 19.6 all-gather.18
  791.1 28.1 reduce-scatter.28
  825.0 19.6 all-gather.20
  938.4 28.1 reduce-scatter.30
  975.3 62.5 reduce-scatter.22
  1041.9 61.5 reduce-scatter.12
  1107.4 61.3 reduce-scatter.14
  1173.0 61.5 reduce-scatter.16
  1238.7 67.8 reduce-scatter.18
  1310.5 68.0 reduce-scatter.20
where the time goes:
time: 1390 us
  waiting for transfers between devices  693 us (50%)
  matrix products  230 us (17%)
  blocking collectives  215 us (15%)
  local copies, waits for them, and re-layouts  150 us (11%)
  other arithmetic  51.5 us (4%)
  loops' own time  28.5 us (2%)
  between operations  17.3 us (1%)
    reduce_scatter x8, waiting for transfers between devices, column_sums(): lax.psum_scatter(partial_terms.astype(jnp.bfloat16), 'tensor', scatter_di...  193 us
    all_gather x8, waiting for transfers between devices, full_rows(): return lax.all_gather(block, 'tensor', axis=0, tiled=True)  150 us
    broadcast_in_dim x24, local copies, waits for them, and re-layouts, block_scores(): masked = jnp.where(mask_block[:, :, None, :, None], scaled, -1000000000.0)  78.5 us
    unnamed x2, blocking collectives  74.9 us
    reduce_scatter x1, waiting for transfers between devices, reduce_grads(): lax.psum_scatter(grads[11], 'dp', scatter_dimension=1, tiled=True)  72 us
    reduce_scatter x1, waiting for transfers between devices, reduce_grads(): lax.psum_scatter(grads[9], 'dp', scatter_dimension=0, tiled=True)  72 us
    reduce_scatter x1, waiting for transfers between devices, reduce_grads(): lax.psum_scatter(grads[3], 'dp', scatter_dimension=0, tiled=True)  65.9 us
    reduce_scatter x1, waiting for transfers between devices, reduce_grads(): lax.psum_scatter(grads[2], 'dp', scatter_dimension=0, tiled=True)  65.3 us
  transfers between devices with their start and end apart: 24, of which 22 were waited for; matrix products, arithmetic and copies ran while one was open for 5% of the time, Pallas kernels for 0%

commit v1 on v0

--- a/solution.py
+++ b/solution.py
@@ -3,6 +3,8 @@
 import jax
 import jax.numpy as jnp
 from jax import lax
+from jax.experimental import pallas as pl
+from jax.experimental.pallas import tpu as pltpu
 from jax.sharding import PartitionSpec as P
 
 HEAD_DIM = 64
@@ -444,9 +446,879 @@
     )
 
 
+MESH = pl.DeviceIdType.MESH
+F32 = jnp.float32
+BF16 = jnp.bfloat16
+LOG2E = 1.4426950408889634
+SCORE_SCALE = HEAD_DIM ** (-0.5)
+TILE = 256
+MESSAGES = 160
+
+
+def dims(left, right, left_dim, right_dim):
+    return lax.dot_general(
+        left, right, (((left_dim,), (right_dim,)), ((), ())), preferred_element_type=F32
+    )
+
+
+def low_lanes(shape):
+    return lax.broadcasted_iota(jnp.int32, shape, len(shape) - 1) < HEAD_DIM
+
+
+def half_turn(block):
+    return pltpu.roll(block.astype(F32), HEAD_DIM, 1).astype(block.dtype)
+
+
+def pairs_of(first, second):
+    tile = lambda pack, index: pack[:, 128 * index : 128 * index + 128]
+    low = low_lanes((first.shape[0], 128))
+    e0, e1, f0, f1 = tile(first, 3), tile(second, 3), tile(first, 4), tile(second, 4)
+    query = (tile(first, 0), tile(second, 0), jnp.where(low, e0, half_turn(e1)))
+    key = (tile(first, 1), tile(second, 1), jnp.where(low, half_turn(e0), e1))
+    value = (tile(first, 2), tile(second, 2), jnp.where(low, f0, half_turn(f1)))
+    out = (tile(first, 5), tile(second, 5), jnp.where(low, half_turn(f0), f1))
+    return query, key, value, out
+
+
+def packs_of(query, key, value, out):
+    low = low_lanes(query[0].shape)
+    first = (
+        query[0],
+        key[0],
+        value[0],
+        jnp.where(low, query[2], half_turn(key[2])),
+        jnp.where(low, value[2], half_turn(out[2])),
+        out[0],
+    )
+    second = (
+        query[1],
+        key[1],
+        value[1],
+        jnp.where(low, half_turn(query[2]), key[2]),
+        jnp.where(low, half_turn(value[2]), out[2]),
+        out[1],
+    )
+    return jnp.concatenate(first, 1), jnp.concatenate(second, 1)
+
+
+def norm_of(values):
+    mean = jnp.mean(values, axis=1, keepdims=True)
+    spread = jnp.mean(values * values, axis=1, keepdims=True) - mean * mean
+    factor = lax.rsqrt(spread + norm_eps)
+    return (values - mean) * factor, factor
+
+
+def norm_pull(upstream, normed, factor, gain):
+    scaled = upstream * gain
+    plain = jnp.mean(scaled, axis=1, keepdims=True)
+    along = jnp.mean(scaled * normed, axis=1, keepdims=True)
+    return factor * (scaled - plain - normed * along)
+
+
+def row_sum(block):
+    return jnp.sum(block, axis=0, keepdims=True)
+
+
+def layer_kernel(
+    pack_ref,
+    vec_ref,
+    mask_ref,
+    in_ref,
+    cot_ref,
+    out_ref,
+    grad_ref,
+    gout_ref,
+    vout_ref,
+    full,
+    vec_z,
+    vec_y,
+    vec_all,
+    masks,
+    tokens,
+    cots,
+    w_in,
+    w_out,
+    bias_q,
+    bias_k,
+    heads,
+    mixed,
+    lse,
+    rows_stat,
+    first_low,
+    feed_low,
+    branch_low,
+    hat_first,
+    fac_first,
+    back_rows,
+    active,
+    slope,
+    inner_buf,
+    send_buf,
+    recv_buf,
+    mixed_back,
+    key_sum,
+    value_sum,
+    heads_back,
+    out_grad,
+    diag_x,
+    diag_y,
+    near_x,
+    near_y,
+    near_z,
+    total,
+    swap_out,
+    swap_in,
+    vgrad,
+    vsend,
+    vrecv,
+    send_sem,
+    recv_sem,
+):
+    dp, tensor = lax.axis_index("dp"), lax.axis_index("tensor")
+    z, y = dp // 2, dp % 2
+    a, b = tensor // 2, tensor % 2
+    core_dev = (dp, tensor + 1 - 2 * b)
+    x_dev = (dp, tensor + 2 - 4 * a)
+    y_dev = (dp + 1 - 2 * y, tensor)
+
+    def z_at(shift):
+        return (z + shift) % 4
+
+    def z_dev(shift):
+        return (z_at(shift) * 2 + y, tensor)
+
+    barrier = pltpu.get_barrier_semaphore()
+    for dev in (core_dev, x_dev, y_dev, z_dev(1), z_dev(2), z_dev(3)):
+        pl.semaphore_signal(barrier, inc=1, device_id=dev, device_id_type=MESH)
+    pl.semaphore_wait(barrier, 6)
+
+    sent = []
+
+    def copy(index, src, dst, dev):
+        return pltpu.make_async_remote_copy(
+            src_ref=src,
+            dst_ref=dst,
+            send_sem=send_sem.at[index],
+            recv_sem=recv_sem.at[index],
+            device_id=dev,
+            device_id_type=MESH,
+        )
+
+    def send(index, src, dst, dev):
+        copy(index, src, dst, dev).start()
+
+    def arrived(index, region, dev=None):
+        copy(index, region, region, core_dev).wait_recv()
+
+    def left(index, region):
+        copy(index, region, region, core_dev).wait_send()
+
+    def piece(side, pack, chip, start=0, size=96):
+        first = pl.multiple_of(chip * 96, 16) + start
+        return full.at[side, pack, pl.ds(pl.multiple_of(first, 16), size), :]
+
+    def gz(pack, j):
+        return pack * 19 + j - 1
+
+    def gx(pack, j):
+        return pack * 19 + 3 + j
+
+    def gy(pack, j):
+        return pack * 19 + 7 + j
+
+    def gdx(pack, j):
+        return pack * 19 + 11 + j
+
+    def gdy(pack, j):
+        return pack * 19 + 15 + j
+
+    def sdx(pack, i):
+        return 57 + pack * 19 + i
+
+    def sdy(pack, i):
+        return 57 + pack * 19 + 4 + i
+
+    def snx(pack, i):
+        return 57 + pack * 19 + 8 + i
+
+    def sny(pack, i):
+        return 57 + pack * 19 + 12 + i
+
+    def snz(pack, i):
+        return 57 + pack * 19 + 15 + i
+
+    M_IN, M_COT, M_MASK, M_VZ, M_VY, M_VX = 114, 115, 116, 117, 120, 121
+    M_TOK, M_OUT, M_GRAD, M_VG = 122, 124, 125, 126
+    M_ROWS, M_PART = 132, 138
+
+    def gather_start(pack):
+        own = pack_ref.at[pack]
+        for j in (1, 3, 2):
+            send(gz(pack, j), own, piece(a, pack, dp), z_dev(j))
+        send(gx(pack, 0), own, piece(a, pack, dp), x_dev)
+        send(gy(pack, 0), own, piece(a, pack, dp), y_dev)
+        full[a, pack, pl.ds(pl.multiple_of(dp * 96, 16), 96), :] = pack_ref[pack]
+
+    def gather_spread(pack, j):
+        spot = piece(a, pack, z_at(-j) * 2 + y)
+        arrived(gz(pack, j), spot)
+        send(gx(pack, j), spot, spot, x_dev)
+        send(gy(pack, j), spot, spot, y_dev)
+
+    def gather_corner(pack, j):
+        from_y = piece(a, pack, z_at(-j) * 2 + 1 - y)
+        arrived(gy(pack, j), from_y)
+        half = piece(a, pack, z_at(-j) * 2 + 1 - y, 0, 48)
+        send(gdx(pack, j), half, half, x_dev)
+        from_x = piece(1 - a, pack, z_at(-j) * 2 + y)
+        arrived(gx(pack, j), from_x)
+        half = piece(1 - a, pack, z_at(-j) * 2 + y, 48, 48)
+        send(gdy(pack, j), half, half, y_dev)
+
+    def gather_end(pack):
+        for j in range(4):
+            arrived(gdx(pack, j), piece(1 - a, pack, z_at(-j) * 2 + 1 - y, 0, 48))
+            arrived(gdy(pack, j), piece(1 - a, pack, z_at(-j) * 2 + 1 - y, 48, 48))
+
+    def gather_left(pack):
+        whole, half = piece(a, pack, dp), piece(a, pack, dp, 0, 48)
+        for j in range(1, 4):
+            left(gz(pack, j), whole)
+        for j in range(4):
+            left(gx(pack, j), whole)
+            left(gy(pack, j), whole)
+            left(gdx(pack, j), half)
+            left(gdy(pack, j), half)
+
+    def scatter_start(pack):
+        for i in (2, 1, 3, 0):
+            chip = z_at(i) * 2 + 1 - y
+            send(sdx(pack, i), piece(1 - a, pack, chip, 0, 48), diag_x.at[pack, i], x_dev)
+            send(sdy(pack, i), piece(1 - a, pack, chip, 48, 48), diag_y.at[pack, i], y_dev)
+
+    def add_to(side, pack, chip, start, size, block):
+        rows = pl.ds(pl.multiple_of(pl.multiple_of(chip * 96, 16) + start, 16), size)
+        full[side, pack, rows, :] = (
+            full[side, pack, rows, :].astype(F32) + block.astype(F32)
+        ).astype(BF16)
+
+    def scatter_near(pack, i):
+        chip = z_at(i) * 2
+        arrived(sdx(pack, i), diag_x.at[pack, i])
+        add_to(a, pack, chip + 1 - y, 0, 48, diag_x[pack, i])
+        send(sny(pack, i), piece(a, pack, chip + 1 - y), near_y.at[pack, i], y_dev)
+        arrived(sdy(pack, i), diag_y.at[pack, i])
+        add_to(1 - a, pack, chip + y, 48, 48, diag_y[pack, i])
+        send(snx(pack, i), piece(1 - a, pack, chip + y), near_x.at[pack, i], x_dev)
+
+    def scatter_line(pack, i):
+        arrived(snx(pack, i), near_x.at[pack, i])
+        arrived(sny(pack, i), near_y.at[pack, i])
+        chip = z_at(i) * 2 + y
+        rows = pl.ds(pl.multiple_of(chip * 96, 16), 96)
+        own = (
+            full[a, pack, rows, :].astype(F32)
+            + near_x[pack, i].astype(F32)
+            + near_y[pack, i].astype(F32)
+        )
+        if i == 0:
+            total[pack] = own
+        else:
+            full[a, pack, rows, :] = own.astype(BF16)
+            send(snz(pack, i), piece(a, pack, chip), near_z.at[pack, i - 1], z_dev(i))
+
+    def scatter_end(pack):
+        own = total[pack]
+        for i in range(1, 4):
+            arrived(snz(pack, i), near_z.at[pack, i - 1])
+            own = own + near_z[pack, i - 1].astype(F32)
+        gout_ref[pack] = own
+
+    def scatter_left(pack):
+        whole, half = piece(a, pack, dp), piece(a, pack, dp, 0, 48)
+        for i in range(4):
+            left(sdx(pack, i), half)
+            left(sdy(pack, i), half)
+            left(snx(pack, i), whole)
+            left(sny(pack, i), whole)
+            if i > 0:
+                left(snz(pack, i), whole)
+
+    send(M_MASK, mask_ref, masks.at[a], x_dev)
+    send(M_IN, in_ref.at[1 - a], tokens.at[tensor], x_dev)
+    for j in range(1, 4):
+        send(M_VZ + j - 1, vec_ref, vec_z.at[j - 1], z_dev(j))
+    gather_start(0)
+    tokens[tensor] = in_ref[a]
+    masks[a] = mask_ref[...]
+    cots[a] = cot_ref[a]
+    send(M_TOK, tokens.at[tensor], tokens.at[tensor], core_dev)
+    vec_own = vec_ref[...].astype(F32)
+    for j in range(1, 4):
+        arrived(M_VZ + j - 1, vec_z.at[j - 1])
+        vec_own = vec_own + vec_z[j - 1].astype(F32)
+    vec_y[0] = vec_own.astype(BF16)
+    send(M_VY, vec_y.at[0], vec_y.at[1], y_dev)
+    gather_spread(0, 1)
+    gather_spread(0, 3)
+    gather_spread(0, 2)
+    arrived(M_VY, vec_y.at[1])
+    vec_all[a] = (vec_own + vec_y[1].astype(F32)).astype(BF16)
+    send(M_VX, vec_all.at[a], vec_all.at[a], x_dev)
+    gather_corner(0, 0)
+    other = (tensor + 2) % 4
+    arrived(M_IN, tokens.at[other])
+    send(M_TOK + 1, tokens.at[other], tokens.at[other], core_dev)
+    gather_corner(0, 1)
+    gather_corner(0, 3)
+    gather_corner(0, 2)
+    gather_start(1)
+    arrived(M_MASK, masks.at[1 - a])
+    spread = (
+        lax.broadcasted_iota(jnp.int32, (128, 16 * BLOCK), 1) // BLOCK
+        == lax.broadcasted_iota(jnp.int32, (128, 16 * BLOCK), 0)
+    )
+    spread = jnp.where(spread, 1.0, 0.0).astype(BF16)
+    for side in range(2):
+        bias = (dims(masks[side], spread, 1, 0) - 1.0) * 1e9
+        for head in range(3):
+            pair, place = (side, head) if head < 2 else (2, side)
+            for part in range(4):
+                start = head * 16 + part * 4
+                bias_q[pair, place, part] = bias[start : start + 4]
+            bias_k[pair, place] = bias[48 + head * 16 : 64 + head * 16]
+    arrived(M_VX, vec_all.at[1 - a])
+    vecs = [vec_all[side].astype(F32) for side in range(2)]
+    arrived(M_TOK, tokens.at[0])
+    arrived(M_TOK + 1, tokens.at[0])
+    gather_end(0)
+
+    def vector(row):
+        return vec_all[0, row : row + 1, :].astype(F32)
+
+    @pl.loop(0, 3)
+    def _(part):
+        rows = pl.ds(pl.multiple_of(part * TILE, TILE), TILE)
+        query, key, value, out = pairs_of(full[0, 0, rows, :], full[1, 0, rows, :])
+        w_in[rows, :] = jnp.concatenate(query + key + value, 1)
+        w_out[rows, :] = jnp.concatenate(out, 1)
+
+    query, key, value, _ = pairs_of(vecs[0], vecs[1])
+    in_bias = jnp.concatenate(query + key + value, 1)[7:8]
+
+    @pl.loop(0, 4)
+    def _(quarter):
+        rows = pl.ds(pl.multiple_of(quarter * TILE, TILE), TILE)
+        for kind in range(3):
+            cols = slice(384 * kind, 384 * kind + 384)
+            block = dims(tokens[quarter], w_in[:, cols], 1, 0) + in_bias[:, cols]
+            block = block.astype(BF16)
+            for pair in range(3):
+                heads[3 * kind + pair, rows, :] = block[:, 128 * pair : 128 * pair + 128]
+
+    gather_spread(1, 1)
+    gather_spread(1, 3)
+    gather_spread(1, 2)
+
+    low = low_lanes((TILE, 128))
+    none = jnp.zeros((TILE, 128), BF16)
+
+    def of_head(block, head):
+        return jnp.where(low, block, none) if head == 0 else jnp.where(low, none, block)
+
+    @pl.loop(0, 12)
+    def _(step):
+        pair, part = step // 4, step % 4
+        rows = pl.ds(pl.multiple_of(part * TILE, TILE), TILE)
+        query_block = heads[pair, rows, :]
+        outs = []
+        for head in range(2):
+            scores = dims(of_head(query_block, head), heads[3 + pair], 1, 1)
+            bias = bias_q[pair, head, part]
+            scores = (
+                scores.reshape(4, BLOCK, 16 * BLOCK) * (SCORE_SCALE * LOG2E)
+                + bias.reshape(4, 1, 16 * BLOCK)
+            ).reshape(TILE, 16 * BLOCK)
+            most = jnp.max(scores, axis=1, keepdims=True)
+            terms = jnp.exp2(scores - most)
+            sums = jnp.sum(terms, axis=1, keepdims=True)
+            outs.append((dims(terms.astype(BF16), heads[6 + pair], 1, 0) / sums, most + jnp.log2(sums)))
+        mixed[pair, rows, :] = jnp.where(low, outs[0][0], outs[1][0]).astype(BF16)
+        lse[pair, rows, :] = jnp.where(low, outs[0][1], outs[1][1])
+
+        @pl.when(step % 3 == 2)
+        def _():
+            gather_corner(1, step // 3)
+
+    gather_start(2)
+
+    def wide(ref, start, count, quarter):
+        rows = pl.ds(pl.multiple_of(quarter * TILE, TILE), TILE)
+        return jnp.concatenate([ref[start + index, rows, :] for index in range(count)], 1)
+
+    def give(number, slot, block):
+        send_buf[number % 2, slot] = block.astype(BF16)
+        index = M_PART + 2 * number + slot
+        send(index, send_buf.at[number % 2, slot], recv_buf.at[number, slot], core_dev)
+
+    def take(number, slot):
+        arrived(M_PART + 2 * number + slot, recv_buf.at[number, slot])
+        return recv_buf[number, slot].astype(F32)
+
+    def given(number):
+        for slot in range(2):
+            left(M_PART + 2 * number + slot, send_buf.at[number % 2, slot])
+
+    def share(kind, slot, ref):
+        spot = ref.at[2 * slot + b]
+        send(M_ROWS + 2 * kind + slot, spot, spot, core_dev)
+
+    def shared(kind, slot, ref):
+        arrived(M_ROWS + 2 * kind + slot, ref.at[2 * slot + 1 - b])
+
+    def branch_part(quarter):
+        return dims(wide(mixed, 0, 3, quarter), w_out[...], 1, 1)
+
+    for slot in range(2):
+        give(0, slot, branch_part(2 * slot + 1 - b))
+    for slot in range(2):
+        quarter = 2 * slot + b
+        own = branch_part(quarter)
+        hidden = tokens[quarter].astype(F32) + own + take(0, slot) + vector(0)
+        normed, factor = norm_of(hidden)
+        hat_first[slot] = normed
+        fac_first[slot] = factor
+        first_low[quarter] = (normed * vector(1) + vector(2)).astype(BF16)
+        share(0, slot, first_low)
+    gather_spread(2, 1)
+    gather_spread(2, 3)
+    gather_spread(2, 2)
+    gather_end(1)
+
+    def feed_up(quarter):
+        for side in range(2):
+            inner_buf[...] = (
+                dims(first_low[quarter], full[side, 1], 1, 0)
+                + vec_all[side, 6:7, :].astype(F32)
+            )
+
+            @pl.loop(0, TILE // 32)
+            def _(chunk):
+                rows = pl.ds(pl.multiple_of(chunk * 32, 32), 32)
+                inner = inner_buf[rows, :]
+                normal = 0.5 * (1.0 + lax.erf(inner * 0.7071067811865476))
+                density = jnp.exp2(inner * inner * (-0.5 * LOG2E)) * 0.3989422804014327
+                active[side, quarter, rows, :] = (inner * normal).astype(BF16)
+                slope[side, quarter, rows, :] = (normal + inner * density).astype(BF16)
+
+    def feed_down(quarter):
+        return dims(active[0, quarter], full[0, 2], 1, 1) + dims(active[1, quarter], full[1, 2], 1, 1)
+
+    feed_up(b)
+    gather_corner(2, 0)
+    gather_corner(2, 1)
+    feed_up(2 + b)
+    gather_corner(2, 3)
+    gather_corner(2, 2)
+    send(M_COT, cot_ref.at[1 - a], cots.at[a], x_dev)
+    for slot in range(2):
+        shared(0, slot, first_low)
+        feed_up(2 * slot + 1 - b)
+    gather_end(2)
+    for slot in range(2):
+        give(1, slot, feed_down(2 * slot + 1 - b))
+    arrived(M_COT, cots.at[1 - a])
+    vgrad[...] = jnp.zeros_like(vgrad)
+    for slot in range(2):
+        quarter = 2 * slot + b
+        own = feed_down(quarter)
+        second_in = hat_first[slot] * vector(1) + vector(2) + own + take(1, slot) + vector(3)
+        normed, factor = norm_of(second_in)
+        swap_out[slot] = (normed * vector(4) + vector(5)).astype(BF16)
+        upstream = cots[slot].astype(F32)
+        back = norm_pull(upstream, normed, factor, vector(4))
+        back_rows[slot] = back
+        feed_low[quarter] = back.astype(BF16)
+        share(1, slot, feed_low)
+        vgrad[0:1, :] += row_sum(upstream * normed)
+        vgrad[1:2, :] += row_sum(upstream)
+        vgrad[2:3, :] += row_sum(back)
+    out_ref[a] = swap_out[a]
+    send(M_OUT, swap_out.at[1 - a], out_ref.at[a], x_dev)
+    for pack in range(3):
+        gather_left(pack)
+
+    def feed_back(quarter):
+        for side in range(2):
+            block = dims(feed_low[quarter], full[side, 2], 1, 0) * slope[side, quarter].astype(F32)
+            inner_low = block.astype(BF16)
+            slope[side, quarter] = inner_low
+            vgrad[6 + side : 7 + side, :] += row_sum(inner_low.astype(F32))
+
+    def rest_back(quarter):
+        return dims(slope[0, quarter], full[0, 1], 1, 1) + dims(slope[1, quarter], full[1, 1], 1, 1)
+
+    def tall(ref, cols):
+        return ref[:, :, cols].reshape(4 * TILE, TILE)
+
+    def weight_grad(pack, left_rows, right_rows):
+        for side_step in range(2):
+            side = 1 - a if side_step == 0 else a
+            right = right_rows[side].reshape(4 * TILE, 768)
+            for part in range(3):
+                block = dims(tall(left_rows, slice(TILE * part, TILE * part + TILE)), right, 0, 0)
+                full[side, pack, TILE * part : TILE * part + TILE, :] = block.astype(BF16)
+
+    feed_back(b)
+    feed_back(2 + b)
+    for slot in range(2):
+        shared(1, slot, feed_low)
+        feed_back(2 * slot + 1 - b)
+    given(0)
+    for slot in range(2):
+        give(2, slot, rest_back(2 * slot + 1 - b))
+    weight_grad(2, feed_low, active)
+    scatter_start(2)
+    for slot in range(2):
+        quarter = 2 * slot + b
+        own = rest_back(quarter)
+        upstream = back_rows[slot] + own + take(2, slot)
+        normed = hat_first[slot]
+        back = norm_pull(upstream, normed, fac_first[slot], vector(1))
+        back_rows[slot] = back
+        branch_low[quarter] = back.astype(BF16)
+        share(2, slot, branch_low)
+        vgrad[3:4, :] += row_sum(upstream * normed)
+        vgrad[4:5, :] += row_sum(upstream)
+        vgrad[5:6, :] += row_sum(back)
+    weight_grad(1, first_low, slope)
+    scatter_start(1)
+
+    for slot in range(2):
+        shared(2, slot, branch_low)
+
+    @pl.loop(0, 4)
+    def _(quarter):
+        rows = pl.ds(pl.multiple_of(quarter * TILE, TILE), TILE)
+        block = dims(branch_low[quarter], w_out[...], 1, 0).astype(BF16)
+        for pair in range(3):
+            mixed_back[pair, rows, :] = block[:, 128 * pair : 128 * pair + 128]
+
+    @pl.loop(0, 12)
+    def _(step):
+        pair, part = step // 4, step % 4
+
+        @pl.when(part == 0)
+        def _():
+            pick = (
+                lax.broadcasted_iota(jnp.int32, (8, 128), 1) // HEAD_DIM
+                == lax.broadcasted_iota(jnp.int32, (8, 128), 0)
+            )
+            pick = jnp.where(pick, 1.0, 0.0).astype(BF16)
+            product = mixed[pair].astype(F32) * mixed_back[pair].astype(F32)
+            high = product.astype(BF16)
+            rest = (product - high.astype(F32)).astype(BF16)
+            rows_stat[0:8, :] = dims(pick, high, 1, 1) + dims(pick, rest, 1, 1)
+            turned = lse[pair].T
+            rows_stat[8:9, :] = turned[0:1]
+            rows_stat[9:10, :] = turned[HEAD_DIM : HEAD_DIM + 1]
+            key_sum[...] = jnp.zeros_like(key_sum)
+            value_sum[...] = jnp.zeros_like(value_sum)
+
+        cols = pl.ds(pl.multiple_of(part * TILE, TILE), TILE)
+        query_block, back_block = heads[pair, cols, :], mixed_back[pair, cols, :]
+        key_block, value_block = heads[3 + pair], heads[6 + pair]
+        key_turned = key_block.T
+        weights, score_backs, queries, backs, query_back = [], [], [], [], []
+        for head in range(2):
+            query_head, back_head = of_head(query_block, head), of_head(back_block, head)
+            scores = dims(key_block, query_head, 1, 1)
+            bias = bias_k[pair, head, :, cols] - rows_stat[8 + head : 9 + head, cols]
+            weight = jnp.exp2(
+                scores.reshape(16, BLOCK, TILE) * (SCORE_SCALE * LOG2E) + bias.reshape(16, 1, TILE)
+            ).reshape(16 * BLOCK, TILE)
+            weight_back = dims(value_block, back_head, 1, 1)
+            score_back = (weight * (weight_back - rows_stat[head : head + 1, cols])).astype(BF16)
+            weights.append(weight.astype(BF16))
+            score_backs.append(score_back)
+            queries.append(query_head)
+            backs.append(back_head)
+            query_back.append(dims(key_turned, score_back, 1, 0))
+        value_sum[...] += dims(jnp.concatenate(weights, 1), jnp.concatenate(backs, 0), 1, 0)
+        key_sum[...] += dims(jnp.concatenate(score_backs, 1), jnp.concatenate(queries, 0), 1, 0)
+        top = lax.broadcasted_iota(jnp.int32, (128, TILE), 0) < HEAD_DIM
+        query_grad = jnp.where(top, query_back[0], query_back[1]).T * SCORE_SCALE
+        heads_back[pair, cols, :] = query_grad.astype(BF16)
+
+        @pl.when(part == 3)
+        def _():
+            heads_back[3 + pair] = (key_sum[...] * SCORE_SCALE).astype(BF16)
+            heads_back[6 + pair] = value_sum[...].astype(BF16)
+
+        @pl.when(part == 3)
+        def _():
+            for i in (2, 1, 3, 0):
+
+                @pl.when(pair == 0)
+                def _():
+                    scatter_near(2, i)
+
+                @pl.when(pair == 1)
+                def _():
+                    scatter_line(2, i)
+                    scatter_near(1, i)
+
+                @pl.when(pair == 2)
+                def _():
+                    scatter_line(1, i)
+
+    for part in range(3):
+        cols = slice(TILE * part, TILE * part + TILE)
+        token_cols = tall(tokens, cols)
+        kinds = []
+        for kind in range(3):
+            right = jnp.concatenate([heads_back[3 * kind + pair] for pair in range(3)], 1)
+            block = dims(token_cols, right, 0, 0)
+            kinds.append(tuple(block[:, 128 * pair : 128 * pair + 128] for pair in range(3)))
+        right = jnp.concatenate([mixed[pair] for pair in range(3)], 1)
+        block = dims(tall(branch_low, cols), right, 0, 0)
+        kinds.append(tuple(block[:, 128 * pair : 128 * pair + 128] for pair in range(3)))
+        first, second = packs_of(*kinds)
+        full[0, 0, cols, :] = first.astype(BF16)
+        full[1, 0, cols, :] = second.astype(BF16)
+    scatter_start(0)
+    for pair in range(3):
+        vgrad[8:9, 128 * pair : 128 * pair + 128] = row_sum(heads_back[pair].astype(F32))
+        vgrad[8:9, 384 + 128 * pair : 512 + 128 * pair] = row_sum(heads_back[6 + pair].astype(F32))
+    send(M_VG, vgrad, vrecv.at[0], core_dev)
+
+    def input_part(quarter):
+        return dims(wide(heads_back, 0, 9, quarter), w_in[...], 1, 1)
+
+    given(1)
+    for slot in range(2):
+        give(3, slot, input_part(2 * slot + 1 - b))
+    arrived(M_VG, vrecv.at[0])
+    mine = lax.broadcasted_iota(jnp.int32, (16, 768), 0) < 6
+    vsend[0] = vgrad[...] + jnp.where(mine, vrecv[0], 0.0)
+    send(M_VG + 1, vsend.at[0], vrecv.at[1], x_dev)
+    for i in (2, 1, 3, 0):
+        scatter_near(0, i)
+    for slot in range(2):
+        own = input_part(2 * slot + b)
+        back_rows[slot] = back_rows[slot] + own + take(3, slot)
+    swap_in[0] = back_rows[1 - a].astype(BF16)
+    send(M_GRAD, swap_in.at[0], swap_in.at[1], x_dev)
+    grad_ref[a] = back_rows[a]
+    arrived(M_VG + 1, vrecv.at[1])
+    vsend[1] = vsend[0] + vrecv[1]
+    send(M_VG + 2, vsend.at[1], vrecv.at[2], y_dev)
+    scatter_end(2)
+    scatter_end(1)
+    arrived(M_VG + 2, vrecv.at[2])
+    vsend[2] = vsend[1] + vrecv[2]
+    for j in range(1, 4):
+        send(M_VG + 2 + j, vsend.at[2], vrecv.at[2 + j], z_dev(j))
+    for i in (2, 1, 3, 0):
+        scatter_line(0, i)
+    every = vsend[2]
+    for j in range(1, 4):
+        arrived(M_VG + 2 + j, vrecv.at[2 + j])
+        every = every + vrecv[2 + j]
+    vout_ref[...] = every
+    arrived(M_GRAD, swap_in.at[1])
+    grad_ref[1 - a] = swap_in[1].astype(F32)
+    arrived(M_OUT, out_ref.at[1 - a])
+    scatter_end(0)
+
+    for pack in range(3):
+        scatter_left(pack)
+    given(2)
+    given(3)
+    left(M_MASK, mask_ref)
+    left(M_IN, in_ref.at[0])
+    left(M_COT, cot_ref.at[0])
+    left(M_OUT, swap_out.at[0])
+    left(M_GRAD, swap_in.at[0])
+    for j in range(3):
+        left(M_VZ + j, vec_ref)
+    left(M_VY, vec_y.at[0])
+    left(M_VX, vec_all.at[0])
+    for slot in range(2):
+        left(M_TOK + slot, tokens.at[0])
+        for kind in range(3):
+            left(M_ROWS + 2 * kind + slot, first_low.at[0])
+    for index in range(6):
+        left(M_VG + index, vsend.at[0])
+
+
+def layer_call(packs, vectors, masks, tokens, cotangent):
+    vmem = pltpu.VMEM
+    anywhere = pl.BlockSpec(memory_space=pltpu.VMEM)
+    shape = jax.ShapeDtypeStruct
+    scratch = [
+        vmem((2, 3, 768, 768), BF16),
+        vmem((3, 16, 768), BF16),
+        vmem((2, 16, 768), BF16),
+        vmem((2, 16, 768), BF16),
+        vmem((2, 96, 128), BF16),
+        vmem((4, TILE, 768), BF16),
+        vmem((2, TILE, 768), BF16),
+        vmem((768, 1152), BF16),
+        vmem((768, 384), BF16),
+        vmem((3, 2, 4, 4, 1024), F32),
+        vmem((3, 2, 16, 1024), F32),
+        vmem((9, 1024, 128), BF16),
+        vmem((3, 1024, 128), BF16),
+        vmem((3, 1024, 128), F32),
+        vmem((16, 1024), F32),
+        vmem((4, TILE, 768), BF16),
+        vmem((4, TILE, 768), BF16),
+        vmem((4, TILE, 768), BF16),
+        vmem((2, TILE, 768), F32),
+        vmem((2, TILE, 1), F32),
+        vmem((2, TILE, 768), F32),
+        vmem((2, 4, TILE, 768), BF16),
+        vmem((2, 4, TILE, 768), BF16),
+        vmem((TILE, 768), F32),
+        vmem((2, 2, TILE, 768), BF16),
+        vmem((4, 2, TILE, 768), BF16),
+        vmem((3, 1024, 128), BF16),
+        vmem((1024, 128), F32),
+        vmem((1024, 128), F32),
+        vmem((9, 1024, 128), BF16),
+        vmem((8, 128), F32),
+        vmem((3, 4, 48, 768), BF16),
+        vmem((3, 4, 48, 768), BF16),
+        vmem((3, 4, 96, 768), BF16),
+        vmem((3, 4, 96, 768), BF16),
+        vmem((3, 3, 96, 768), BF16),
+        vmem((3, 96, 768), F32),
+        vmem((2, TILE, 768), BF16),
+        vmem((2, TILE, 768), BF16),
+        vmem((16, 768), F32),
+        vmem((3, 16, 768), F32),
+        vmem((6, 16, 768), F32),
+        pltpu.SemaphoreType.DMA((MESSAGES,)),
+        pltpu.SemaphoreType.DMA((MESSAGES,)),
+    ]
+    return pl.pallas_call(
+        layer_kernel,
+        out_shape=(
+            shape(tokens.shape, BF16),
+            shape(tokens.shape, F32),
+            shape(packs.shape, F32),
+            shape(vectors.shape, F32),
+        ),
+        in_specs=[anywhere] * 5,
+        out_specs=(anywhere,) * 4,
+        scratch_shapes=scratch,
+        compiler_params=pltpu.CompilerParams(
+            collective_id=0, has_side_effects=True, vmem_limit_bytes=62 << 20
+        ),
+    )(packs, vectors, masks, tokens, cotangent)
+
+
+def local_fast(
+    inputs,
+    random_blocks,
+    query_weight,
+    query_bias,
+    key_weight,
+    value_weight,
+    value_bias,
+    out_weight,
+    out_bias,
+    first_gain,
+    first_shift,
+    up_weight,
+    up_bias,
+    down_weight,
+    down_bias,
+    second_gain,
+    second_shift,
+    cotangent,
+):
+    dp, tensor = lax.axis_index("dp"), lax.axis_index("tensor")
+    out_turned = out_weight.T
+    first_pack = jnp.concatenate(
+        (
+            query_weight[:, :128],
+            key_weight[:, :128],
+            value_weight[:, :128],
+            query_weight[:, 128:],
+            key_weight[:, 128:],
+            value_weight[:, 128:],
+            out_turned[:, 128:],
+            out_turned[:, :128],
+        ),
+        1,
+    )
+    packs = jnp.stack((first_pack, up_weight, down_weight.T))
+
+    def placed(values):
+        width = values.shape[0]
+        spots = jnp.arange(8 * width, dtype=jnp.int32) // width
+        return jnp.where(spots == dp, jnp.tile(values, 8), jnp.zeros((), values.dtype))
+
+    query_row, value_row = placed(query_bias), placed(value_bias)
+    gap = jnp.zeros((128,), BF16)
+    in_row = jnp.concatenate(
+        (query_row[:128], gap, value_row[:128], query_row[128:], gap[:64], value_row[128:], gap, gap[:64])
+    )
+    rows = [
+        placed(v) for v in (out_bias, first_gain, first_shift, down_bias, second_gain, second_shift, up_bias)
+    ]
+    vectors = jnp.concatenate((jnp.stack(rows + [in_row]), jnp.zeros((8, 768), BF16)))
+    allowed = block_allowed(random_blocks, random_blocks.shape[1]).astype(BF16)
+    masks = jnp.concatenate((allowed.reshape(48, 16), allowed.transpose(0, 2, 1).reshape(48, 16)))
+    masks = jnp.pad(masks, ((0, 0), (0, 112)))
+    output, input_grad, grads, sums = layer_call(packs, vectors, masks, inputs, cotangent)
+    first = grads[0]
+    query_grad = jnp.concatenate((first[:, 0:128], first[:, 384:448]), 1)
+    key_grad = jnp.concatenate((first[:, 128:256], first[:, 448:512]), 1)
+    value_grad = jnp.concatenate((first[:, 256:384], first[:, 512:576]), 1)
+    out_grad = jnp.concatenate((first[:, 640:768], first[:, 576:640]), 1).T
+    side = tensor // 2
+
+    def own(row):
+        return lax.dynamic_slice(row, (dp * 96,), (96,))
+
+    def head_bias(row):
+        both = jnp.concatenate(
+            (
+                lax.dynamic_slice(row, (side * 128,), (128,)),
+                lax.dynamic_slice(row, (256 + side * 64,), (64,)),
+            )
+        )
+        return lax.dynamic_slice(both, (dp * 24,), (24,))
+
+    return (
+        output,
+        input_grad,
+        query_grad,
+        head_bias(sums[8, :384]),
+        key_grad,
+        value_grad,
+        head_bias(sums[8, 384:]),
+        out_grad,
+        own(sums[5]),
+        own(sums[3]),
+        own(sums[4]),
+        grads[1],
+        own(lax.dynamic_slice(sums, (6 + side, 0), (1, 768))[0]),
+        grads[2].T,
+        own(sums[2]),
+        own(sums[0]),
+        own(sums[1]),
+    )
+
+
 def solution(mesh):
+    sizes = mesh.shape
+    fast = sizes["dp"] == 8 and sizes["tensor"] == 4
     return jax.shard_map(
-        local,
+        local_fast if fast else local,
         mesh=mesh,
         in_specs=(
             P("dp", "tensor", None),

time: 1390 us -> 210 us (0.15)
  waiting for transfers between devices: 693 us -> 0 us
  matrix products: 230 us -> 0 us
  blocking collectives: 215 us -> 0 us
  Pallas kernels: 0 us -> 182 us
  local copies, waits for them, and re-layouts: 150 us -> 20.8 us
  other arithmetic: 51.5 us -> 4.75 us
  loops' own time: 28.5 us -> 0 us
  between operations: 17.3 us -> 1.05 us
    reduce_scatter x13 -> x0, waiting for transfers between devices: 533 us -> none  [the longest x8 193 us: column_sums(): lax.psum_scatter(partial_terms.astype(jnp.bfloat16), 'tensor', scatter_di...]
    dot_general x64 -> x0, matrix products: 230 us -> none  [the longest x4 39.6 us: one_part(): jnp.einsum('hqk,qhd->khd', scores_back, query_block, preferred_element_ty...]
    pallas_call x0 -> x1, Pallas kernels: none -> 182 us  [layer_call(): pl.pallas_call(layer_kernel, out_shape=(shape(tokens.shape, BF16), shape(...]
    all_gather x10 -> x0, waiting for transfers between devices: 150 us -> none  [the longest x8 150 us: full_rows(): return lax.all_gather(block, 'tensor', axis=0, tiled=True)]
    all_gather x4 -> x0, blocking collectives: 133 us -> none  [the longest x1 33.5 us: gather_weights(): lax.all_gather(shards[5], 'dp', axis=1, tiled=True)]
    broadcast_in_dim x24 -> x2, local copies, waits for them, and re-layouts: 78.5 us -> 0.01 us  [the longest x1 0.01 us: local_fast(): jnp.zeros((8, 768), BF16)]
    unnamed x2 -> x0, blocking collectives: 74.9 us -> none
    while x374 -> x0, local copies, waits for them, and re-layouts: 37.6 us -> none
  transfers between devices with their start and end apart: 24 -> 0, of which waited for: 22 -> 0; matrix products, arithmetic and copies ran while one was open for 5% -> 0% of each run, Pallas kernels for 0% -> 0%
where the time goes in v1:
time: 210 us; the launch traced here: 209 us
  Pallas kernels  182 us (87%)
  local copies, waits for them, and re-layouts  20.8 us (10%)
  other arithmetic  4.75 us (2%)
    pallas_call x1, Pallas kernels, layer_call(): pl.pallas_call(layer_kernel, out_shape=(shape(tokens.shape, BF16), shape(...  182 us
    dynamic_slice x7, local copies, waits for them, and re-layouts, own(): return lax.dynamic_slice(row, (dp * 96,), (96,))  4.77 us

profile of v1, /device:TPU:0, one launch (start us, length us, event | category | flops | bytes accessed | tf_op | source)
XLA Modules:
  0.0 208.9 jit_solution(17537739441968507853)
XLA Ops:
  0.7 0.0 copy-start.3
  0.7 0.0 copy-start.4
  0.7 0.0 copy-start.5
  0.7 0.0 copy-start.6
  0.7 0.0 copy-start.7
  0.7 0.0 copy-start.8
  0.7 0.0 copy-start.9
  0.7 0.0 copy-start.10
  0.7 0.0 copy-start.11
  0.7 0.0 copy-start.2
  0.8 0.8 slice.93
  1.6 0.7 slice.94
  2.3 0.7 slice.95
  3.0 0.7 slice.96
  3.8 0.7 slice.97
  4.5 0.7 slice.98
  5.3 0.9 copy.52
  6.2 0.1 concatenate.31
  6.3 1.8 pad_maximum_fusion.pack_ref
  8.1 0.0 copy-done.3
  8.1 0.1 tile.37
  8.2 0.1 tile.41
  8.3 0.1 tile.39
  8.4 0.0 copy-done.6
  8.4 0.1 tile.90
  8.5 0.0 copy-done.7
  8.5 0.1 tile.43
  8.7 0.1 tile.94
  8.8 0.1 tile.92
  8.9 0.1 tile.98
  9.0 0.1 tile.96
  9.2 0.1 concatenate.32
  9.3 1.2 concatenate.33.vec_ref
  10.5 0.1 fusion
  10.6 0.1 fusion.4
  10.7 0.1 reshape.268
  10.8 0.1 copy.53
  10.9 0.1 copy.58
  11.0 0.1 pad_add_fusion
  11.1 0.1 copy.56
  11.2 0.6 pad_convert_fusion.mask_ref
  11.8 182.3 %shard_map.305 = (bf16[2,256,768]{2,1,0:T(8,128)(2,1)}, f32[2,256,768]{2,1,0:T(8,128)}, f32[3,96,768]{2,1,0:T(8,128)}, f32[16,768]{1,0:T(8,128)}) custom-call(bf16[3,96,768]{2,1,0:T(8,128)(2,1)} %pad_maximum_fusion.pack_ref, bf16[16,768]{1,0:T(8,128)(2,1)} %concatenate.33.vec_ref, bf16[96,128]{1,0:T(8,128)(2,1)} %pad_convert_fusion.mask_ref, ...), custom_call_target="tpu_custom_call" | custom-call | tf_op jit(solution)/shard_map/pallas_call | solution.py:1205
  194.2 2.1 slice_bitcast_fusion
  196.3 0.1 fusion.24
  196.4 0.0 copy-start
  196.4 0.6 pad_maximum_fusion.1
  197.0 0.7 fusion.26
  197.8 0.1 fusion.12
  197.8 0.6 dynamic_slice.66
  198.4 0.6 pad_maximum_fusion.2
  199.1 0.6 pad_maximum_fusion.3
  199.7 0.1 fusion.14
  199.8 0.6 dynamic_slice.71
  200.4 0.7 copy.57
  201.2 1.0 fusion.25
  202.1 0.6 fusion.15
  202.7 0.6 fusion.16
  203.3 0.6 fusion.17
  203.9 1.3 dynamic-slice_bitcast_fusion
  205.2 0.6 fusion.18
  205.7 0.6 fusion.19
  206.3 0.6 fusion.20
  206.9 0.9 copy.61
  207.8 1.1 copy.62
  (42 shorter events, 0.3 us)
Async XLA Ops:
  0.7 7.4 %copy-start.3 = (bf16[96]{0:T(256)(128)(2,1)S(1)}, bf16[96]{0:T(256)(128)(2,1)}, u32[]{:S(2)}) copy-start(bf16[96]{0:T(256)(128)(2,1)} %param.26) | copy-start | bytes 580
  0.7 7.5 %copy-start.4 = (bf16[96]{0:T(256)(128)(2,1)S(1)}, bf16[96]{0:T(256)(128)(2,1)}, u32[]{:S(2)}) copy-start(bf16[96]{0:T(256)(128)(2,1)} %param.28) | copy-start | bytes 580
  0.7 7.6 %copy-start.5 = (bf16[96]{0:T(256)(128)(2,1)S(1)}, bf16[96]{0:T(256)(128)(2,1)}, u32[]{:S(2)}) copy-start(bf16[96]{0:T(256)(128)(2,1)} %param.27) | copy-start | bytes 580
  0.7 7.7 %copy-start.6 = (bf16[96]{0:T(256)(128)(2,1)S(1)}, bf16[96]{0:T(256)(128)(2,1)}, u32[]{:S(2)}) copy-start(bf16[96]{0:T(256)(128)(2,1)} %param.33) | copy-start | bytes 580
  0.7 7.8 %copy-start.7 = (bf16[96]{0:T(256)(128)(2,1)S(1)}, bf16[96]{0:T(256)(128)(2,1)}, u32[]{:S(2)}) copy-start(bf16[96]{0:T(256)(128)(2,1)} %param.32) | copy-start | bytes 580
  0.7 7.9 %copy-start.8 = (bf16[96]{0:T(256)(128)(2,1)S(1)}, bf16[96]{0:T(256)(128)(2,1)}, u32[]{:S(2)}) copy-start(bf16[96]{0:T(256)(128)(2,1)} %param.30) | copy-start | bytes 580
  0.7 8.0 %copy-start.9 = (bf16[96]{0:T(256)(128)(2,1)S(1)}, bf16[96]{0:T(256)(128)(2,1)}, u32[]{:S(2)}) copy-start(bf16[96]{0:T(256)(128)(2,1)} %param.34) | copy-start | bytes 580
  0.7 8.2 %copy-start.10 = (bf16[24]{0:T(256)(128)(2,1)S(1)}, bf16[24]{0:T(256)(128)(2,1)}, u32[]{:S(2)}) copy-start(bf16[24]{0:T(256)(128)(2,1)} %param.24) | copy-start | bytes 148
  0.7 8.3 %copy-start.11 = (bf16[24]{0:T(256)(128)(2,1)S(1)}, bf16[24]{0:T(256)(128)(2,1)}, u32[]{:S(2)}) copy-start(bf16[24]{0:T(256)(128)(2,1)} %param.21) | copy-start | bytes 148
  0.7 9.8 %copy-start.2 = (s32[3,16,3]{1,2,0:T(4,128)S(1)}, s32[3,16,3]{1,2,0:T(4,128)}, u32[]{:S(2)}) copy-start(s32[3,16,3]{1,2,0:T(4,128)} %param.19) | copy-start | bytes 1732
  194.2 12.7 %copy-start.1 = (bf16[2,256,768]{2,1,0:T(8,128)(2,1)S(1)}, bf16[2,256,768]{2,1,0:T(8,128)(2,1)}, u32[]{:S(2)}) copy-start(bf16[2,256,768]{2,1,0:T(8,128)(2,1)} %get-tuple-element.141) | copy-start | bytes 2359300
  196.4 11.4 %copy-start = (f32[2,256,768]{2,1,0:T(8,128)S(1)}, f32[2,256,768]{2,1,0:T(8,128)}, u32[]{:S(2)}) copy-start(f32[2,256,768]{2,1,0:T(8,128)} %get-tuple-element.142) | copy-start | bytes 4718596

commit v2 on v1

--- a/solution.py
+++ b/solution.py
@@ -447,12 +447,218 @@
 
 
 MESH = pl.DeviceIdType.MESH
+(
+    START,
+    SPREAD,
+    OVER_Y,
+    OVER_X,
+    DEEP,
+    BACK_DEEP,
+    BACK_Y,
+    BACK_X,
+    BACK_LINE,
+    COT,
+) = range(10)
+PLAN = {
+    "pre": (
+        (START, 1, 0),
+        (OVER_Y, 0, 0),
+        (SPREAD, 0, 1),
+        (OVER_Y, 1, 0),
+        (SPREAD, 0, 2),
+    ),
+    "tok": (
+        (SPREAD, 0, 3),
+        (SPREAD, 1, 1),
+        (OVER_X, 1, 0),
+    ),
+    "p0": (
+        (OVER_X, 0, 1),
+        (SPREAD, 1, 2),
+        (OVER_X, 0, 0),
+        (DEEP, 0, 0),
+        (OVER_Y, 0, 3),
+        (OVER_X, 0, 2),
+        (OVER_Y, 0, 2),
+        (OVER_Y, 0, 1),
+        (START, 2, 0),
+        (OVER_X, 0, 3),
+        (OVER_Y, 1, 2),
+        (DEEP, 1, 0),
+        (START, 3, 0),
+        (OVER_X, 1, 1),
+        (OVER_X, 1, 2),
+    ),
+    "q0": (
+        (SPREAD, 1, 3),
+        (SPREAD, 2, 1),
+    ),
+    "q1": (
+        (OVER_Y, 2, 0),
+        (SPREAD, 2, 3),
+        (OVER_X, 1, 3),
+        (OVER_Y, 1, 3),
+        (DEEP, 2, 0),
+        (OVER_Y, 1, 1),
+    ),
+    "f1": (
+        (OVER_X, 2, 0),
+        (OVER_X, 2, 1),
+        (SPREAD, 2, 2),
+    ),
+    "f3": (
+        (OVER_Y, 2, 1),
+        (OVER_X, 2, 3),
+    ),
+    "f4": (
+        (COT, 0, 0),
+    ),
+    "f7": (
+        (OVER_X, 3, 0),
+    ),
+    "p1": (
+        (SPREAD, 3, 1),
+    ),
+    "f9": (
+        (OVER_X, 2, 2),
+    ),
+    "f10": (
+        (OVER_Y, 2, 3),
+        (OVER_Y, 3, 0),
+        (SPREAD, 3, 3),
+    ),
+    "f11": (
+        (OVER_Y, 2, 2),
+        (SPREAD, 3, 2),
+    ),
+    "b0": (
+        (OVER_X, 3, 1),
+        (OVER_Y, 3, 1),
+    ),
+    "b1": (
+        (OVER_Y, 3, 3),
+    ),
+    "u0": (
+        (OVER_X, 3, 3),
+    ),
+    "u1": (
+        (OVER_X, 3, 2),
+        (DEEP, 3, 0),
+        (OVER_Y, 3, 2),
+    ),
+    "r0": (
+        (BACK_X, 3, 2),
+        (BACK_Y, 3, 3),
+        (BACK_Y, 3, 2),
+        (BACK_X, 4, 3),
+        (BACK_X, 3, 3),
+        (BACK_X, 4, 1),
+        (BACK_DEEP, 3, 0),
+        (BACK_Y, 4, 3),
+        (BACK_X, 3, 1),
+        (BACK_Y, 4, 1),
+    ),
+    "r1": (
+        (BACK_LINE, 3, 2),
+        (BACK_X, 4, 2),
+        (BACK_DEEP, 4, 0),
+    ),
+    "r2": (
+        (BACK_X, 3, 0),
+        (BACK_X, 4, 0),
+        (BACK_Y, 3, 1),
+        (BACK_LINE, 3, 3),
+        (BACK_Y, 3, 0),
+    ),
+    "r3": (
+        (BACK_Y, 4, 2),
+        (BACK_Y, 4, 0),
+    ),
+    "k0": (
+        (BACK_LINE, 4, 3),
+    ),
+    "k1": (
+        (BACK_X, 2, 2),
+        (BACK_X, 2, 3),
+    ),
+    "k2": (
+        (BACK_LINE, 3, 1),
+    ),
+    "k3": (
+        (BACK_LINE, 4, 1),
+        (BACK_Y, 2, 2),
+        (BACK_LINE, 4, 2),
+    ),
+    "k4": (
+        (BACK_X, 2, 1),
+        (BACK_DEEP, 2, 0),
+    ),
+    "k5": (
+        (BACK_Y, 2, 1),
+        (BACK_Y, 2, 3),
+    ),
+    "k7": (
+        (BACK_LINE, 2, 2),
+        (BACK_Y, 2, 0),
+    ),
+    "k8": (
+        (BACK_Y, 0, 2),
+        (BACK_X, 2, 0),
+    ),
+    "k9": (
+        (BACK_Y, 0, 3),
+        (BACK_X, 0, 2),
+    ),
+    "k10": (
+        (BACK_X, 0, 1),
+    ),
+    "k11": (
+        (BACK_X, 0, 3),
+    ),
+    "t0": (
+        (BACK_LINE, 3, 0),
+        (BACK_LINE, 4, 0),
+        (BACK_DEEP, 0, 0),
+    ),
+    "t1": (
+        (BACK_LINE, 0, 2),
+        (BACK_LINE, 2, 1),
+        (BACK_Y, 0, 1),
+        (BACK_LINE, 2, 3),
+        (BACK_X, 1, 2),
+        (BACK_X, 1, 3),
+        (BACK_Y, 1, 1),
+        (BACK_X, 0, 0),
+        (BACK_X, 1, 1),
+        (BACK_LINE, 2, 0),
+        (BACK_Y, 1, 3),
+    ),
+    "t2": (
+        (BACK_LINE, 0, 1),
+        (BACK_Y, 1, 2),
+        (BACK_LINE, 1, 1),
+        (BACK_LINE, 0, 3),
+        (BACK_Y, 0, 0),
+        (BACK_LINE, 1, 2),
+        (BACK_LINE, 1, 3),
+        (BACK_DEEP, 1, 0),
+        (BACK_LINE, 0, 0),
+    ),
+    "t3": (
+        (BACK_X, 1, 0),
+        (BACK_Y, 1, 0),
+        (BACK_LINE, 1, 0),
+    ),
+}
 F32 = jnp.float32
 BF16 = jnp.bfloat16
 LOG2E = 1.4426950408889634
 SCORE_SCALE = HEAD_DIM ** (-0.5)
 TILE = 256
-MESSAGES = 160
+MESSAGES = 272
+LEAN = 16
+TURN = 32
+BEND = 48
 
 
 def dims(left, right, left_dim, right_dim):
@@ -472,31 +678,29 @@
 def pairs_of(first, second):
     tile = lambda pack, index: pack[:, 128 * index : 128 * index + 128]
     low = low_lanes((first.shape[0], 128))
-    e0, e1, f0, f1 = tile(first, 3), tile(second, 3), tile(first, 4), tile(second, 4)
-    query = (tile(first, 0), tile(second, 0), jnp.where(low, e0, half_turn(e1)))
-    key = (tile(first, 1), tile(second, 1), jnp.where(low, half_turn(e0), e1))
-    value = (tile(first, 2), tile(second, 2), jnp.where(low, f0, half_turn(f1)))
-    out = (tile(first, 5), tile(second, 5), jnp.where(low, half_turn(f0), f1))
-    return query, key, value, out
-
-
-def packs_of(query, key, value, out):
-    low = low_lanes(query[0].shape)
+    e0, e1, f0, f1 = tile(first, 0), tile(second, 0), tile(first, 1), tile(second, 1)
+    third = (
+        jnp.where(low, e0, half_turn(e1)),
+        jnp.where(low, half_turn(e0), e1),
+        jnp.where(low, f0, half_turn(f1)),
+    )
+    out = (tile(first, 2), tile(second, 2), jnp.where(low, half_turn(f0), f1))
+    return jnp.concatenate(third, 1), jnp.concatenate(out, 1)
+
+
+def packs_of(third, out):
+    tile = lambda block, index: block[:, 128 * index : 128 * index + 128]
+    query, key, value = (tile(third, index) for index in range(3))
+    low = low_lanes(query.shape)
     first = (
-        query[0],
-        key[0],
-        value[0],
-        jnp.where(low, query[2], half_turn(key[2])),
-        jnp.where(low, value[2], half_turn(out[2])),
-        out[0],
+        jnp.where(low, query, half_turn(key)),
+        jnp.where(low, value, half_turn(tile(out, 2))),
+        tile(out, 0),
     )
     second = (
-        query[1],
-        key[1],
-        value[1],
-        jnp.where(low, half_turn(query[2]), key[2]),
-        jnp.where(low, half_turn(value[2]), out[2]),
-        out[1],
+        jnp.where(low, half_turn(query), key),
+        jnp.where(low, half_turn(value), tile(out, 2)),
+        tile(out, 1),
     )
     return jnp.concatenate(first, 1), jnp.concatenate(second, 1)
 
@@ -520,31 +724,46 @@
 
 
 def layer_kernel(
-    pack_ref,
-    vec_ref,
-    mask_ref,
+    query_ref,
+    key_ref,
+    value_ref,
+    down_ref,
+    up_ref,
+    project_ref,
+    row_refs,
+    query_bias_ref,
+    value_bias_ref,
+    picks_ref,
     in_ref,
     cot_ref,
     out_ref,
     grad_ref,
-    gout_ref,
+    gout_half,
+    gout_wide,
     vout_ref,
-    full,
+    pack_ref,
+    vec_ref,
+    mask_ref,
+    half,
+    wide,
     vec_z,
     vec_y,
     vec_all,
     masks,
     tokens,
+    tokens_turned,
     cots,
     w_in,
     w_out,
     bias_q,
     bias_k,
     heads,
+    keys_turned,
     mixed,
     lse,
-    rows_stat,
+    centre,
     first_low,
+    first_turned,
     feed_low,
     branch_low,
     hat_first,
@@ -565,9 +784,9 @@
     near_x,
     near_y,
     near_z,
+    deep_z,
     total,
     swap_out,
-    swap_in,
     vgrad,
     vsend,
     vrecv,
@@ -592,8 +811,6 @@
         pl.semaphore_signal(barrier, inc=1, device_id=dev, device_id_type=MESH)
     pl.semaphore_wait(barrier, 6)
 
-    sent = []
-
     def copy(index, src, dst, dev):
         return pltpu.make_async_remote_copy(
             src_ref=src,
@@ -607,143 +824,297 @@
     def send(index, src, dst, dev):
         copy(index, src, dst, dev).start()
 
-    def arrived(index, region, dev=None):
+    def arrived(index, region):
         copy(index, region, region, core_dev).wait_recv()
 
     def left(index, region):
         copy(index, region, region, core_dev).wait_send()
 
+    def store(pack):
+        return (half, wide)[pack // 2], pack % 2
+
+    def chip_rows(chip, start=0, size=96):
+        first = pl.multiple_of(chip * 96, 16) + start
+        return pl.ds(pl.multiple_of(first, 16), size)
+
     def piece(side, pack, chip, start=0, size=96):
-        first = pl.multiple_of(chip * 96, 16) + start
-        return full.at[side, pack, pl.ds(pl.multiple_of(first, 16), size), :]
-
-    def gz(pack, j):
-        return pack * 19 + j - 1
-
-    def gx(pack, j):
-        return pack * 19 + 3 + j
-
-    def gy(pack, j):
-        return pack * 19 + 7 + j
-
-    def gdx(pack, j):
-        return pack * 19 + 11 + j
-
-    def gdy(pack, j):
-        return pack * 19 + 15 + j
-
-    def sdx(pack, i):
-        return 57 + pack * 19 + i
-
-    def sdy(pack, i):
-        return 57 + pack * 19 + 4 + i
-
-    def snx(pack, i):
-        return 57 + pack * 19 + 8 + i
-
-    def sny(pack, i):
-        return 57 + pack * 19 + 12 + i
-
-    def snz(pack, i):
-        return 57 + pack * 19 + 15 + i
-
-    M_IN, M_COT, M_MASK, M_VZ, M_VY, M_VX = 114, 115, 116, 117, 120, 121
-    M_TOK, M_OUT, M_GRAD, M_VG = 122, 124, 125, 126
-    M_ROWS, M_PART = 132, 138
+        ref, slot = store(pack)
+        return ref.at[side, slot, chip_rows(chip, start, size), :]
+
+    def back_store(pack):
+        if pack == 2:
+            return wide, 0, slice(0, 768)
+        if pack > 2:
+            return half, pack - 3, slice(0, 384)
+        return wide, 1, slice(384 * pack, 384 * pack + 384)
+
+    def back_piece(side, pack, chip, start=0, size=96):
+        ref, slot, cols = back_store(pack)
+        return ref.at[side, slot, chip_rows(chip, start, size), cols]
+
+    def part_of(refs, pack):
+        return refs[1].at[0] if pack == 2 else refs[0].at[(0, 1, None, 2, 3)[pack]]
+
+    def gather_id(pack, kind, j):
+        return pack * 28 + 4 * kind + j
+
+    def scatter_id(pack, kind, i):
+        return 112 + pack * 24 + 4 * kind + i
+
+    M_IN, M_COT, M_MASK, M_VZ, M_VY, M_VX = 232, 233, 234, 235, 238, 239
+    M_TOK, M_OUT, M_GRAD, M_VG = 240, 242, 243, 244
+    M_ROWS, M_PART = 250, 256
+    Z_OWN, X_NEAR, Y_NEAR, X_CORNER, Y_CORNER, Z_X, Z_Y = range(7)
+
+    def corner_id(pack, j):
+        return gather_id(pack, (Z_OWN, Z_X, Z_Y)[j - 1], 0)
+
+    D_X, D_Y, N_X, N_Y, L_Z, Q_Z = range(6)
 
     def gather_start(pack):
-        own = pack_ref.at[pack]
+        own = (pack_ref.at[0], pack_ref.at[1], up_ref, down_ref)[pack]
         for j in (1, 3, 2):
-            send(gz(pack, j), own, piece(a, pack, dp), z_dev(j))
-        send(gx(pack, 0), own, piece(a, pack, dp), x_dev)
-        send(gy(pack, 0), own, piece(a, pack, dp), y_dev)
-        full[a, pack, pl.ds(pl.multiple_of(dp * 96, 16), 96), :] = pack_ref[pack]
+            send(gather_id(pack, Z_OWN, j), own, piece(a, pack, dp), z_dev(j))
+        send(gather_id(pack, X_NEAR, 0), own, piece(a, pack, dp), x_dev)
+        send(gather_id(pack, Y_NEAR, 0), own, piece(a, pack, dp), y_dev)
+        ref, slot = store(pack)
+        ref[a, slot, chip_rows(dp), :] = own[...]
 
     def gather_spread(pack, j):
-        spot = piece(a, pack, z_at(-j) * 2 + y)
-        arrived(gz(pack, j), spot)
-        send(gx(pack, j), spot, spot, x_dev)
-        send(gy(pack, j), spot, spot, y_dev)
-
-    def gather_corner(pack, j):
-        from_y = piece(a, pack, z_at(-j) * 2 + 1 - y)
-        arrived(gy(pack, j), from_y)
-        half = piece(a, pack, z_at(-j) * 2 + 1 - y, 0, 48)
-        send(gdx(pack, j), half, half, x_dev)
-        from_x = piece(1 - a, pack, z_at(-j) * 2 + y)
-        arrived(gx(pack, j), from_x)
-        half = piece(1 - a, pack, z_at(-j) * 2 + y, 48, 48)
-        send(gdy(pack, j), half, half, y_dev)
+        chip = z_at(-j) * 2 + y
+        arrived(gather_id(pack, Z_OWN, j), piece(a, pack, chip))
+        spot = piece(a, pack, chip, LEAN, 96 - LEAN)
+        send(gather_id(pack, X_NEAR, j), spot, spot, x_dev)
+        send(gather_id(pack, Y_NEAR, j), spot, spot, y_dev)
+
+    def gather_over_y(pack, j):
+        first = 0 if j == 0 else LEAN
+        chip = z_at(-j) * 2 + 1 - y
+        arrived(gather_id(pack, Y_NEAR, j), piece(a, pack, chip, first, 96 - first))
+        spot = piece(a, pack, chip, first, TURN - first)
+        send(gather_id(pack, X_CORNER, j), spot, spot, x_dev)
+        if j == 0:
+            for step in (1, 3, 2):
+                spot = piece(a, pack, chip, 0, LEAN)
+                send(gather_id(pack, Z_Y, step), spot, spot, z_dev(step))
+
+    def gather_over_x(pack, j):
+        first = 0 if j == 0 else LEAN
+        chip = z_at(-j) * 2 + y
+        arrived(gather_id(pack, X_NEAR, j), piece(1 - a, pack, chip, first, 96 - first))
+        spot = piece(1 - a, pack, chip, TURN, 96 - TURN)
+        send(gather_id(pack, Y_CORNER, j), spot, spot, y_dev)
+        if j == 0:
+            for step in (1, 3, 2):
+                spot = piece(1 - a, pack, chip, 0, LEAN)
+                send(gather_id(pack, Z_X, step), spot, spot, z_dev(step))
+
+    def gather_deep(pack, _):
+        chip = z * 2 + 1 - y
+        arrived(gather_id(pack, X_CORNER, 0), piece(1 - a, pack, chip, 0, TURN))
+        spot = piece(1 - a, pack, chip, 0, LEAN)
+        for step in (1, 3, 2):
+            send(corner_id(pack, step), spot, spot, z_dev(step))
 
     def gather_end(pack):
         for j in range(4):
-            arrived(gdx(pack, j), piece(1 - a, pack, z_at(-j) * 2 + 1 - y, 0, 48))
-            arrived(gdy(pack, j), piece(1 - a, pack, z_at(-j) * 2 + 1 - y, 48, 48))
+            over_y, over_x = z_at(-j) * 2 + 1 - y, z_at(-j) * 2 + y
+            arrived(gather_id(pack, Y_CORNER, j), piece(1 - a, pack, over_y, TURN, 96 - TURN))
+            if j > 0:
+                arrived(gather_id(pack, X_CORNER, j), piece(1 - a, pack, over_y, LEAN, TURN - LEAN))
+                arrived(gather_id(pack, Z_Y, j), piece(a, pack, over_y, 0, LEAN))
+                arrived(gather_id(pack, Z_X, j), piece(1 - a, pack, over_x, 0, LEAN))
+                arrived(corner_id(pack, j), piece(1 - a, pack, over_y, 0, LEAN))
 
     def gather_left(pack):
-        whole, half = piece(a, pack, dp), piece(a, pack, dp, 0, 48)
-        for j in range(1, 4):
-            left(gz(pack, j), whole)
+        def rows(size):
+            return piece(a, pack, dp, 0, size)
+
         for j in range(4):
-            left(gx(pack, j), whole)
-            left(gy(pack, j), whole)
-            left(gdx(pack, j), half)
-            left(gdy(pack, j), half)
+            first = 0 if j == 0 else LEAN
+            left(gather_id(pack, X_NEAR, j), rows(96 - first))
+            left(gather_id(pack, Y_NEAR, j), rows(96 - first))
+            left(gather_id(pack, X_CORNER, j), rows(TURN - first))
+            left(gather_id(pack, Y_CORNER, j), rows(96 - TURN))
+            if j > 0:
+                left(gather_id(pack, Z_OWN, j), rows(96))
+                left(gather_id(pack, Z_Y, j), rows(LEAN))
+                left(gather_id(pack, Z_X, j), rows(LEAN))
+                left(corner_id(pack, j), rows(LEAN))
+
+    def add_to(side, pack, chip, start, *blocks):
+        ref, slot, cols = back_store(pack)
+        rows = chip_rows(chip, start, blocks[0].shape[0])
+        summed = ref[side, slot, rows, cols].astype(F32)
+        for block in blocks:
+            summed = summed + block.astype(F32)
+        ref[side, slot, rows, cols] = summed.astype(BF16)
+
+    def scatter_corner(pack, i):
+        first = 0 if i == 0 else LEAN
+        chip = z_at(i) * 2 + 1 - y
+        over_x = part_of(diag_x, pack).at[i, pl.ds(0, BEND - first), :]
+        send(scatter_id(pack, D_X, i), back_piece(1 - a, pack, chip, first, BEND - first), over_x, x_dev)
+        over_y = part_of(diag_y, pack).at[i]
+        send(scatter_id(pack, D_Y, i), back_piece(1 - a, pack, chip, BEND, 96 - BEND), over_y, y_dev)
+
+    def scatter_first(pack):
+        for i in (2, 1, 3):
+            scatter_corner(pack, i)
 
     def scatter_start(pack):
-        for i in (2, 1, 3, 0):
-            chip = z_at(i) * 2 + 1 - y
-            send(sdx(pack, i), piece(1 - a, pack, chip, 0, 48), diag_x.at[pack, i], x_dev)
-            send(sdy(pack, i), piece(1 - a, pack, chip, 48, 48), diag_y.at[pack, i], y_dev)
-
-    def add_to(side, pack, chip, start, size, block):
-        rows = pl.ds(pl.multiple_of(pl.multiple_of(chip * 96, 16) + start, 16), size)
-        full[side, pack, rows, :] = (
-            full[side, pack, rows, :].astype(F32) + block.astype(F32)
-        ).astype(BF16)
-
-    def scatter_near(pack, i):
-        chip = z_at(i) * 2
-        arrived(sdx(pack, i), diag_x.at[pack, i])
-        add_to(a, pack, chip + 1 - y, 0, 48, diag_x[pack, i])
-        send(sny(pack, i), piece(a, pack, chip + 1 - y), near_y.at[pack, i], y_dev)
-        arrived(sdy(pack, i), diag_y.at[pack, i])
-        add_to(1 - a, pack, chip + y, 48, 48, diag_y[pack, i])
-        send(snx(pack, i), piece(1 - a, pack, chip + y), near_x.at[pack, i], x_dev)
+        for i in (2, 1, 3):
+            for side in range(2):
+                for line in range(2):
+                    spot = back_piece(side, pack, z_at(i) * 2 + line, 0, LEAN)
+                    slot = part_of(deep_z, pack).at[i - 1, 2 * side + line]
+                    send(scatter_id(pack, Q_Z, i), spot, slot, z_dev(i))
+
+    def scatter_deep(pack, _):
+        parts = part_of(deep_z, pack)
+        for i in range(1, 4):
+            arrived(scatter_id(pack, Q_Z, i), parts.at[i - 1])
+        for side in range(2):
+            for line in range(2):
+                terms = [parts[i, 2 * side + line] for i in range(3)]
+                add_to(side, pack, z * 2 + line, 0, *terms)
+        scatter_corner(pack, 0)
+
+    def scatter_near_y(pack, i):
+        first = 0 if i == 0 else LEAN
+        chip = z_at(i) * 2 + 1 - y
+        over_x = part_of(diag_x, pack).at[i, pl.ds(0, BEND - first), :]
+        arrived(scatter_id(pack, D_X, i), over_x)
+        add_to(a, pack, chip, first, over_x[...])
+        spot = back_piece(a, pack, chip, first, 96 - first)
+        goal = part_of(near_y, pack).at[i, pl.ds(0, 96 - first), :]
+        send(scatter_id(pack, N_Y, i), spot, goal, y_dev)
+
+    def scatter_near_x(pack, i):
+        first = 0 if i == 0 else LEAN
+        chip = z_at(i) * 2 + y
+        over_y = part_of(diag_y, pack).at[i]
+        arrived(scatter_id(pack, D_Y, i), over_y)
+        add_to(1 - a, pack, chip, BEND, over_y[...])
+        spot = back_piece(1 - a, pack, chip, first, 96 - first)
+        goal = part_of(near_x, pack).at[i, pl.ds(0, 96 - first), :]
+        send(scatter_id(pack, N_X, i), spot, goal, x_dev)
 
     def scatter_line(pack, i):
-        arrived(snx(pack, i), near_x.at[pack, i])
-        arrived(sny(pack, i), near_y.at[pack, i])
+        first = 0 if i == 0 else LEAN
+        size = 96 - first
+        from_x = part_of(near_x, pack).at[i, pl.ds(0, size), :]
+        from_y = part_of(near_y, pack).at[i, pl.ds(0, size), :]
+        arrived(scatter_id(pack, N_X, i), from_x)
+        arrived(scatter_id(pack, N_Y, i), from_y)
         chip = z_at(i) * 2 + y
-        rows = pl.ds(pl.multiple_of(chip * 96, 16), 96)
-        own = (
-            full[a, pack, rows, :].astype(F32)
-            + near_x[pack, i].astype(F32)
-            + near_y[pack, i].astype(F32)
-        )
+        ref, slot, cols = back_store(pack)
+        rows = chip_rows(chip, first, size)
+        own = ref[a, slot, rows, cols].astype(F32) + from_x[...].astype(F32) + from_y[...].astype(F32)
         if i == 0:
-            total[pack] = own
+            part_of(total, pack)[...] = own
         else:
-            full[a, pack, rows, :] = own.astype(BF16)
-            send(snz(pack, i), piece(a, pack, chip), near_z.at[pack, i - 1], z_dev(i))
+            ref[a, slot, rows, cols] = own.astype(BF16)
+            spot = back_piece(a, pack, chip, first, size)
+            send(scatter_id(pack, L_Z, i), spot, part_of(near_z, pack).at[i - 1], z_dev(i))
 
     def scatter_end(pack):
-        own = total[pack]
+        parts, sums = part_of(near_z, pack), part_of(total, pack)
         for i in range(1, 4):
-            arrived(snz(pack, i), near_z.at[pack, i - 1])
-            own = own + near_z[pack, i - 1].astype(F32)
-        gout_ref[pack] = own
+            arrived(scatter_id(pack, L_Z, i), parts.at[i - 1])
+        goal = part_of((gout_half, gout_wide), pack)
+        goal[0:LEAN, :] = sums[0:LEAN, :]
+        own = sums[LEAN:96, :]
+        for i in range(3):
+            own = own + parts[i].astype(F32)
+        goal[LEAN:96, :] = own
 
     def scatter_left(pack):
-        whole, half = piece(a, pack, dp), piece(a, pack, dp, 0, 48)
+        def rows(size):
+            return back_piece(a, pack, dp, 0, size)
+
         for i in range(4):
-            left(sdx(pack, i), half)
-            left(sdy(pack, i), half)
-            left(snx(pack, i), whole)
-            left(sny(pack, i), whole)
+            first = 0 if i == 0 else LEAN
+            left(scatter_id(pack, D_X, i), rows(BEND - first))
+            left(scatter_id(pack, D_Y, i), rows(96 - BEND))
+            left(scatter_id(pack, N_X, i), rows(96 - first))
+            left(scatter_id(pack, N_Y, i), rows(96 - first))
             if i > 0:
-                left(snz(pack, i), whole)
-
+                left(scatter_id(pack, L_Z, i), rows(96 - LEAN))
+                left(scatter_id(pack, Q_Z, i), rows(4 * LEAN))
+
+    def send_cot(pack, _):
+        send(M_COT, cot_ref.at[1 - a], cots.at[a], x_dev)
+
+    moves = (
+        lambda pack, _: gather_start(pack),
+        gather_spread,
+        gather_over_y,
+        gather_over_x,
+        gather_deep,
+        scatter_deep,
+        scatter_near_y,
+        scatter_near_x,
+        scatter_line,
+        send_cot,
+    )
+
+    def run(label):
+        for kind, pack, place in PLAN.get(label, ()):
+            moves[kind](pack, place)
+
+    def run_at(step, prefix, count):
+        for index in range(count):
+            if PLAN.get(prefix + str(index)):
+                pl.when(step == index)(lambda: run(prefix + str(index)))
+
+    def turned(ref):
+        block = ref[...].astype(F32)
+        gap = jnp.zeros((block.shape[0], 128 - block.shape[1]), F32)
+        return jnp.concatenate((block, gap), 1).T[: block.shape[1], :].astype(BF16)
+
+    def placed(rows, width):
+        gap = jnp.zeros((rows.shape[0], width - rows.shape[1]), F32)
+        return pltpu.roll(jnp.concatenate((rows, gap), 1), dp * rows.shape[1], 1)
+
+    project = turned(project_ref)
+    pack_ref[0] = jnp.concatenate((query_ref[:, :128], key_ref[:, :128], value_ref[:, :128]), 1)
+    pack_ref[1] = jnp.concatenate(
+        (
+            query_ref[:, 128:],
+            key_ref[:, 128:],
+            value_ref[:, 128:],
+            project[:, 128:],
+            project[:, :128],
+        ),
+        1,
+    )
+    rows = jnp.concatenate([ref[...].reshape(1, 96).astype(F32) for ref in row_refs], 0)
+    query_row = placed(query_bias_ref[...].reshape(1, 24).astype(F32), 256)
+    value_row = placed(value_bias_ref[...].reshape(1, 24).astype(F32), 256)
+    gap = jnp.zeros((1, 128), F32)
+    in_row = jnp.concatenate(
+        (query_row[:, :128], gap, value_row[:, :128], query_row[:, 128:], value_row[:, 128:], gap), 1
+    )
+    vec_ref[...] = jnp.concatenate((placed(rows, 768), in_row, jnp.zeros((8, 768), F32)), 0).astype(
+        BF16
+    )
+    column = lax.broadcasted_iota(jnp.int32, (16, 128), 1)
+    row = lax.broadcasted_iota(jnp.int32, (16, 128), 0)
+    fixed = (
+        ((column - row <= 1) & (row - column <= 1))
+        | (column == 0)
+        | (column == 15)
+        | (row == 0)
+        | (row == 15)
+    )
+    for head in range(3):
+        allowed = fixed
+        for pick in range(picks_ref.shape[1]):
+            picks = picks_ref[head, pick : pick + 1, :]
+            picks = jnp.concatenate((picks, jnp.full((1, 112), -1, jnp.int32)), 1)
+            allowed = allowed | (picks == row)
+        mask_ref[16 * head : 16 * head + 16, :] = jnp.where(allowed, 1.0, 0.0).astype(BF16)
     send(M_MASK, mask_ref, masks.at[a], x_dev)
     send(M_IN, in_ref.at[1 - a], tokens.at[tensor], x_dev)
     for j in range(1, 4):
@@ -759,20 +1130,6 @@
         vec_own = vec_own + vec_z[j - 1].astype(F32)
     vec_y[0] = vec_own.astype(BF16)
     send(M_VY, vec_y.at[0], vec_y.at[1], y_dev)
-    gather_spread(0, 1)
-    gather_spread(0, 3)
-    gather_spread(0, 2)
-    arrived(M_VY, vec_y.at[1])
-    vec_all[a] = (vec_own + vec_y[1].astype(F32)).astype(BF16)
-    send(M_VX, vec_all.at[a], vec_all.at[a], x_dev)
-    gather_corner(0, 0)
-    other = (tensor + 2) % 4
-    arrived(M_IN, tokens.at[other])
-    send(M_TOK + 1, tokens.at[other], tokens.at[other], core_dev)
-    gather_corner(0, 1)
-    gather_corner(0, 3)
-    gather_corner(0, 2)
-    gather_start(1)
     arrived(M_MASK, masks.at[1 - a])
     spread = (
         lax.broadcasted_iota(jnp.int32, (128, 16 * BLOCK), 1) // BLOCK
@@ -783,87 +1140,110 @@
         bias = (dims(masks[side], spread, 1, 0) - 1.0) * 1e9
         for head in range(3):
             pair, place = (side, head) if head < 2 else (2, side)
+            bias_k[pair, place] = bias[16 * head : 16 * head + 16]
+            rows = masks[side, 16 * head : 16 * head + 16, :]
+            turned_bias = (dims(rows, spread[:16], 0, 0) - 1.0) * 1e9
             for part in range(4):
-                start = head * 16 + part * 4
-                bias_q[pair, place, part] = bias[start : start + 4]
-            bias_k[pair, place] = bias[48 + head * 16 : 64 + head * 16]
-    arrived(M_VX, vec_all.at[1 - a])
-    vecs = [vec_all[side].astype(F32) for side in range(2)]
+                bias_q[pair, place, part] = turned_bias[4 * part : 4 * part + 4]
+    run("pre")
+    arrived(M_VY, vec_y.at[1])
+    vec_all[a] = (vec_own + vec_y[1].astype(F32)).astype(BF16)
+    send(M_VX, vec_all.at[a], vec_all.at[a], x_dev)
+    other = (tensor + 2) % 4
+    arrived(M_IN, tokens.at[other])
+    send(M_TOK + 1, tokens.at[other], tokens.at[other], core_dev)
+    run("tok")
+
+    def vector(row):
+        return vec_all[0, row : row + 1, :].astype(F32)
+
+    def turn_rows(goal, ref, quarter):
+        cols = pl.ds(pl.multiple_of(quarter * TILE, TILE), TILE)
+        goal[:, cols] = ref[quarter].astype(F32).T.astype(BF16)
+
     arrived(M_TOK, tokens.at[0])
     arrived(M_TOK + 1, tokens.at[0])
-    gather_end(0)
-
-    def vector(row):
-        return vec_all[0, row : row + 1, :].astype(F32)
-
-    @pl.loop(0, 3)
-    def _(part):
-        rows = pl.ds(pl.multiple_of(part * TILE, TILE), TILE)
-        query, key, value, out = pairs_of(full[0, 0, rows, :], full[1, 0, rows, :])
-        w_in[rows, :] = jnp.concatenate(query + key + value, 1)
-        w_out[rows, :] = jnp.concatenate(out, 1)
-
-    query, key, value, _ = pairs_of(vecs[0], vecs[1])
-    in_bias = jnp.concatenate(query + key + value, 1)[7:8]
 
     @pl.loop(0, 4)
     def _(quarter):
-        rows = pl.ds(pl.multiple_of(quarter * TILE, TILE), TILE)
-        for kind in range(3):
-            cols = slice(384 * kind, 384 * kind + 384)
-            block = dims(tokens[quarter], w_in[:, cols], 1, 0) + in_bias[:, cols]
-            block = block.astype(BF16)
-            for pair in range(3):
-                heads[3 * kind + pair, rows, :] = block[:, 128 * pair : 128 * pair + 128]
-
-    gather_spread(1, 1)
-    gather_spread(1, 3)
-    gather_spread(1, 2)
+        turn_rows(tokens_turned, tokens, quarter)
+
+    def project_heads(pair, bias):
+        @pl.loop(0, 4)
+        def _(quarter):
+            rows = pl.ds(pl.multiple_of(quarter * TILE, TILE), TILE)
+            block = dims(tokens[quarter], w_in[pair], 1, 0) + bias
+            for kind in range(3):
+                tile = block[:, 128 * kind : 128 * kind + 128]
+                heads[3 * kind + pair, rows, :] = tile.astype(BF16)
+                if kind == 1:
+                    keys_turned[pair, :, rows] = tile.T.astype(BF16)
+
+    run("p0")
+    gather_end(0)
+    arrived(M_VX, vec_all.at[1 - a])
+    for side in range(2):
+        w_in[side] = half[side, 0]
+        project_heads(side, vec_all[side, 7:8, 0:384].astype(F32))
+        run("q" + str(side))
+
+    def third_heads():
+        run("p1")
+        gather_end(1)
+
+        @pl.loop(0, 3)
+        def _(part):
+            rows = pl.ds(pl.multiple_of(part * TILE, TILE), TILE)
+            third, out = pairs_of(half[0, 1, rows, :], half[1, 1, rows, :])
+            w_in[2, rows, :] = third
+            w_out[rows, :] = out
+
+        vecs = [vec_all[side, :, 384:768].astype(F32) for side in range(2)]
+        project_heads(2, pairs_of(vecs[0], vecs[1])[0][7:8])
 
     low = low_lanes((TILE, 128))
     none = jnp.zeros((TILE, 128), BF16)
+    top = lax.broadcasted_iota(jnp.int32, (128, TILE), 0) < HEAD_DIM
 
     def of_head(block, head):
         return jnp.where(low, block, none) if head == 0 else jnp.where(low, none, block)
 
     @pl.loop(0, 12)
     def _(step):
+        pl.when(step == 8)(third_heads)
         pair, part = step // 4, step % 4
-        rows = pl.ds(pl.multiple_of(part * TILE, TILE), TILE)
-        query_block = heads[pair, rows, :]
-        outs = []
+        cols = pl.ds(pl.multiple_of(part * TILE, TILE), TILE)
+        query_block = heads[pair, cols, :]
+        terms, sums, mosts = [], [], []
         for head in range(2):
-            scores = dims(of_head(query_block, head), heads[3 + pair], 1, 1)
-            bias = bias_q[pair, head, part]
-            scores = (
-                scores.reshape(4, BLOCK, 16 * BLOCK) * (SCORE_SCALE * LOG2E)
-                + bias.reshape(4, 1, 16 * BLOCK)
-            ).reshape(TILE, 16 * BLOCK)
+            scores = dims(of_head(query_block, head), heads[3 + pair], 1, 1).reshape(4, BLOCK, 1024)
+            bias = bias_q[pair, head, part].reshape(4, 1, 1024)
+            scores = (scores * (SCORE_SCALE * LOG2E) + bias).reshape(TILE, 1024)
             most = jnp.max(scores, axis=1, keepdims=True)
-            terms = jnp.exp2(scores - most)
-            sums = jnp.sum(terms, axis=1, keepdims=True)
-            outs.append((dims(terms.astype(BF16), heads[6 + pair], 1, 0) / sums, most + jnp.log2(sums)))
-        mixed[pair, rows, :] = jnp.where(low, outs[0][0], outs[1][0]).astype(BF16)
-        lse[pair, rows, :] = jnp.where(low, outs[0][1], outs[1][1])
-
-        @pl.when(step % 3 == 2)
-        def _():
-            gather_corner(1, step // 3)
-
-    gather_start(2)
-
-    def wide(ref, start, count, quarter):
+            term = jnp.exp2(scores - most)
+            sums.append(jnp.sum(term, axis=1, keepdims=True))
+            terms.append(term.astype(BF16))
+            mosts.append(most)
+        both = dims(jnp.concatenate(terms, 0), heads[6 + pair], 1, 0)
+        mixed[pair, cols, :] = jnp.where(low, both[:TILE] / sums[0], both[TILE:] / sums[1]).astype(BF16)
+        totals = [most + jnp.log2(total) for most, total in zip(mosts, sums)]
+        turned_totals = jnp.where(low, totals[0], totals[1]).T
+        lse[pair, 0, :, cols] = turned_totals[0:1]
+        lse[pair, 1, :, cols] = turned_totals[HEAD_DIM : HEAD_DIM + 1]
+        run_at(step, "f", 12)
+
+    def beside(ref, indices, quarter):
         rows = pl.ds(pl.multiple_of(quarter * TILE, TILE), TILE)
-        return jnp.concatenate([ref[start + index, rows, :] for index in range(count)], 1)
+        return jnp.concatenate([ref[index, rows, :] for index in indices], 1)
 
     def give(number, slot, block):
         send_buf[number % 2, slot] = block.astype(BF16)
         index = M_PART + 2 * number + slot
-        send(index, send_buf.at[number % 2, slot], recv_buf.at[number, slot], core_dev)
+        send(index, send_buf.at[number % 2, slot], recv_buf.at[number % 2, slot], core_dev)
 
     def take(number, slot):
-        arrived(M_PART + 2 * number + slot, recv_buf.at[number, slot])
-        return recv_buf[number, slot].astype(F32)
+        arrived(M_PART + 2 * number + slot, recv_buf.at[number % 2, slot])
+        return recv_buf[number % 2, slot].astype(F32)
 
     def given(number):
         for slot in range(2):
@@ -877,11 +1257,16 @@
         arrived(M_ROWS + 2 * kind + slot, ref.at[2 * slot + 1 - b])
 
     def branch_part(quarter):
-        return dims(wide(mixed, 0, 3, quarter), w_out[...], 1, 1)
-
-    for slot in range(2):
+        return dims(beside(mixed, range(3), quarter), w_out[...], 1, 1)
+
+    @pl.loop(0, 2)
+    def _(slot):
         give(0, slot, branch_part(2 * slot + 1 - b))
-    for slot in range(2):
+
+    run("b0")
+
+    @pl.loop(0, 2)
+    def _(slot):
         quarter = 2 * slot + b
         own = branch_part(quarter)
         hidden = tokens[quarter].astype(F32) + own + take(0, slot) + vector(0)
@@ -890,15 +1275,18 @@
         fac_first[slot] = factor
         first_low[quarter] = (normed * vector(1) + vector(2)).astype(BF16)
         share(0, slot, first_low)
-    gather_spread(2, 1)
-    gather_spread(2, 3)
-    gather_spread(2, 2)
-    gather_end(1)
+
+    run("b1")
+    for slot in range(2):
+        turn_rows(first_turned, first_low, 2 * slot + b)
+    run("b2")
+    gather_end(2)
 
     def feed_up(quarter):
-        for side in range(2):
+        @pl.loop(0, 2)
+        def _(side):
             inner_buf[...] = (
-                dims(first_low[quarter], full[side, 1], 1, 0)
+                dims(first_low[quarter], wide[side, 0], 1, 0)
                 + vec_all[side, 6:7, :].astype(F32)
             )
 
@@ -912,24 +1300,27 @@
                 slope[side, quarter, rows, :] = (normal + inner * density).astype(BF16)
 
     def feed_down(quarter):
-        return dims(active[0, quarter], full[0, 2], 1, 1) + dims(active[1, quarter], full[1, 2], 1, 1)
+        return dims(active[0, quarter], wide[0, 1], 1, 1) + dims(active[1, quarter], wide[1, 1], 1, 1)
 
     feed_up(b)
-    gather_corner(2, 0)
-    gather_corner(2, 1)
+    run("u0")
     feed_up(2 + b)
-    gather_corner(2, 3)
-    gather_corner(2, 2)
-    send(M_COT, cot_ref.at[1 - a], cots.at[a], x_dev)
+    run("u1")
     for slot in range(2):
         shared(0, slot, first_low)
         feed_up(2 * slot + 1 - b)
-    gather_end(2)
-    for slot in range(2):
+        run("u" + str(2 + slot))
+    gather_end(3)
+
+    @pl.loop(0, 2)
+    def _(slot):
         give(1, slot, feed_down(2 * slot + 1 - b))
+
     arrived(M_COT, cots.at[1 - a])
     vgrad[...] = jnp.zeros_like(vgrad)
-    for slot in range(2):
+
+    @pl.loop(0, 2)
+    def _(slot):
         quarter = 2 * slot + b
         own = feed_down(quarter)
         second_in = hat_first[slot] * vector(1) + vector(2) + own + take(1, slot) + vector(3)
@@ -943,43 +1334,63 @@
         vgrad[0:1, :] += row_sum(upstream * normed)
         vgrad[1:2, :] += row_sum(upstream)
         vgrad[2:3, :] += row_sum(back)
+
     out_ref[a] = swap_out[a]
     send(M_OUT, swap_out.at[1 - a], out_ref.at[a], x_dev)
-    for pack in range(3):
+    for pack in range(4):
         gather_left(pack)
 
     def feed_back(quarter):
         for side in range(2):
-            block = dims(feed_low[quarter], full[side, 2], 1, 0) * slope[side, quarter].astype(F32)
+            block = dims(feed_low[quarter], wide[side, 1], 1, 0) * slope[side, quarter].astype(F32)
             inner_low = block.astype(BF16)
             slope[side, quarter] = inner_low
             vgrad[6 + side : 7 + side, :] += row_sum(inner_low.astype(F32))
 
     def rest_back(quarter):
-        return dims(slope[0, quarter], full[0, 1], 1, 1) + dims(slope[1, quarter], full[1, 1], 1, 1)
+        return dims(slope[0, quarter], wide[0, 0], 1, 1) + dims(slope[1, quarter], wide[1, 0], 1, 1)
 
     def tall(ref, cols):
         return ref[:, :, cols].reshape(4 * TILE, TILE)
 
-    def weight_grad(pack, left_rows, right_rows):
-        for side_step in range(2):
-            side = 1 - a if side_step == 0 else a
-            right = right_rows[side].reshape(4 * TILE, 768)
-            for part in range(3):
-                block = dims(tall(left_rows, slice(TILE * part, TILE * part + TILE)), right, 0, 0)
-                full[side, pack, TILE * part : TILE * part + TILE, :] = block.astype(BF16)
-
-    feed_back(b)
-    feed_back(2 + b)
+    sides = (1 - a, a)
+
+    def down_grad(side, part):
+        @pl.loop(0, 3)
+        def _(piece_rows):
+            rows = pl.ds(pl.multiple_of(piece_rows * TILE, TILE), TILE)
+            right = active[side, :, :, 384 * part : 384 * part + 384].reshape(4 * TILE, 384)
+            half[side, part, rows, :] = dims(tall(feed_low, rows), right, 0, 0).astype(BF16)
+
+
+    @pl.loop(0, 2)
+    def _(slot):
+        feed_back(2 * slot + b)
+
     for slot in range(2):
         shared(1, slot, feed_low)
+    for part in range(2):
+        down_grad(sides[0], part)
+        scatter_first(3 + part)
+        down_grad(sides[1], part)
+        scatter_start(3 + part)
+
+    @pl.loop(0, 2)
+    def _(slot):
         feed_back(2 * slot + 1 - b)
+
     given(0)
+
+    @pl.loop(0, 2)
+    def _(slot):
+        give(2, slot, rest_back(2 * slot + 1 - b))
+
     for slot in range(2):
-        give(2, slot, rest_back(2 * slot + 1 - b))
-    weight_grad(2, feed_low, active)
-    scatter_start(2)
-    for slot in range(2):
+        turn_rows(first_turned, first_low, 2 * slot + 1 - b)
+    run("r0")
+
+    @pl.loop(0, 2)
+    def _(slot):
         quarter = 2 * slot + b
         own = rest_back(quarter)
         upstream = back_rows[slot] + own + take(2, slot)
@@ -991,8 +1402,18 @@
         vgrad[3:4, :] += row_sum(upstream * normed)
         vgrad[4:5, :] += row_sum(upstream)
         vgrad[5:6, :] += row_sum(back)
-    weight_grad(1, first_low, slope)
-    scatter_start(1)
+
+    run("r1")
+    for side in sides:
+        @pl.loop(0, 3)
+        def _(part):
+            rows = pl.ds(pl.multiple_of(part * TILE, TILE), TILE)
+            right = slope[side].reshape(4 * TILE, 768)
+            wide[side, 0, rows, :] = dims(first_turned[rows, :], right, 1, 0).astype(BF16)
+        if side is sides[0]:
+            scatter_first(2)
+    scatter_start(2)
+    run("r2")
 
     for slot in range(2):
         shared(2, slot, branch_low)
@@ -1003,6 +1424,25 @@
         block = dims(branch_low[quarter], w_out[...], 1, 0).astype(BF16)
         for pair in range(3):
             mixed_back[pair, rows, :] = block[:, 128 * pair : 128 * pair + 128]
+
+    run("r3")
+
+    @pl.loop(0, 3)
+    def _(part):
+        rows = pl.ds(pl.multiple_of(part * TILE, TILE), TILE)
+        right = jnp.concatenate([mixed[pair] for pair in range(3)], 1)
+        out_grad[rows, :] = dims(tall(branch_low, rows), right, 0, 0).astype(BF16)
+    run("r4")
+
+    def heads_grad(pair, rows):
+        right = jnp.concatenate([heads_back[3 * kind + pair] for kind in range(3)], 1)
+        return dims(tokens_turned[rows, :], right, 1, 0)
+
+    def first_heads_grad(side):
+        @pl.loop(0, 3)
+        def _(part):
+            rows = pl.ds(pl.multiple_of(part * TILE, TILE), TILE)
+            wide[side, 1, rows, 0:384] = heads_grad(side, rows).astype(BF16)
 
     @pl.loop(0, 12)
     def _(step):
@@ -1018,35 +1458,29 @@
             product = mixed[pair].astype(F32) * mixed_back[pair].astype(F32)
             high = product.astype(BF16)
             rest = (product - high.astype(F32)).astype(BF16)
-            rows_stat[0:8, :] = dims(pick, high, 1, 1) + dims(pick, rest, 1, 1)
-            turned = lse[pair].T
-            rows_stat[8:9, :] = turned[0:1]
-            rows_stat[9:10, :] = turned[HEAD_DIM : HEAD_DIM + 1]
+            centre[...] = dims(pick, high, 1, 1) + dims(pick, rest, 1, 1)
             key_sum[...] = jnp.zeros_like(key_sum)
             value_sum[...] = jnp.zeros_like(value_sum)
 
         cols = pl.ds(pl.multiple_of(part * TILE, TILE), TILE)
         query_block, back_block = heads[pair, cols, :], mixed_back[pair, cols, :]
-        key_block, value_block = heads[3 + pair], heads[6 + pair]
-        key_turned = key_block.T
+        value_block = heads[6 + pair]
         weights, score_backs, queries, backs, query_back = [], [], [], [], []
         for head in range(2):
             query_head, back_head = of_head(query_block, head), of_head(back_block, head)
-            scores = dims(key_block, query_head, 1, 1)
-            bias = bias_k[pair, head, :, cols] - rows_stat[8 + head : 9 + head, cols]
-            weight = jnp.exp2(
-                scores.reshape(16, BLOCK, TILE) * (SCORE_SCALE * LOG2E) + bias.reshape(16, 1, TILE)
-            ).reshape(16 * BLOCK, TILE)
+            bias = bias_k[pair, head, :, cols] - lse[pair, head, :, cols]
+            scores = dims(heads[3 + pair], query_head, 1, 1).reshape(16, BLOCK, TILE)
+            scores = scores * (SCORE_SCALE * LOG2E) + bias.reshape(16, 1, TILE)
+            weight = jnp.exp2(scores.reshape(1024, TILE))
             weight_back = dims(value_block, back_head, 1, 1)
-            score_back = (weight * (weight_back - rows_stat[head : head + 1, cols])).astype(BF16)
+            score_back = (weight * (weight_back - centre[head : head + 1, cols])).astype(BF16)
             weights.append(weight.astype(BF16))
             score_backs.append(score_back)
             queries.append(query_head)
             backs.append(back_head)
-            query_back.append(dims(key_turned, score_back, 1, 0))
+            query_back.append(dims(keys_turned[pair], score_back, 1, 0))
         value_sum[...] += dims(jnp.concatenate(weights, 1), jnp.concatenate(backs, 0), 1, 0)
         key_sum[...] += dims(jnp.concatenate(score_backs, 1), jnp.concatenate(queries, 0), 1, 0)
-        top = lax.broadcasted_iota(jnp.int32, (128, TILE), 0) < HEAD_DIM
         query_grad = jnp.where(top, query_back[0], query_back[1]).T * SCORE_SCALE
         heads_back[pair, cols, :] = query_grad.astype(BF16)
 
@@ -1055,83 +1489,88 @@
             heads_back[3 + pair] = (key_sum[...] * SCORE_SCALE).astype(BF16)
             heads_back[6 + pair] = value_sum[...].astype(BF16)
 
-        @pl.when(part == 3)
+        @pl.when(step == 7)
         def _():
-            for i in (2, 1, 3, 0):
-
-                @pl.when(pair == 0)
-                def _():
-                    scatter_near(2, i)
-
-                @pl.when(pair == 1)
-                def _():
-                    scatter_line(2, i)
-                    scatter_near(1, i)
-
-                @pl.when(pair == 2)
-                def _():
-                    scatter_line(1, i)
-
-    for part in range(3):
-        cols = slice(TILE * part, TILE * part + TILE)
-        token_cols = tall(tokens, cols)
-        kinds = []
-        for kind in range(3):
-            right = jnp.concatenate([heads_back[3 * kind + pair] for pair in range(3)], 1)
-            block = dims(token_cols, right, 0, 0)
-            kinds.append(tuple(block[:, 128 * pair : 128 * pair + 128] for pair in range(3)))
-        right = jnp.concatenate([mixed[pair] for pair in range(3)], 1)
-        block = dims(tall(branch_low, cols), right, 0, 0)
-        kinds.append(tuple(block[:, 128 * pair : 128 * pair + 128] for pair in range(3)))
-        first, second = packs_of(*kinds)
-        full[0, 0, cols, :] = first.astype(BF16)
-        full[1, 0, cols, :] = second.astype(BF16)
-    scatter_start(0)
+            for side in range(2):
+                first_heads_grad(side)
+            scatter_first(0)
+            scatter_start(0)
+
+        run_at(step, "k", 12)
+
+    @pl.loop(0, 3)
+    def _(part):
+        rows = pl.ds(pl.multiple_of(part * TILE, TILE), TILE)
+        first, second = packs_of(heads_grad(2, rows), out_grad[rows, :].astype(F32))
+        wide[0, 1, rows, 384:768] = first.astype(BF16)
+        wide[1, 1, rows, 384:768] = second.astype(BF16)
+
+    scatter_first(1)
+    scatter_start(1)
+    run("t0")
     for pair in range(3):
         vgrad[8:9, 128 * pair : 128 * pair + 128] = row_sum(heads_back[pair].astype(F32))
         vgrad[8:9, 384 + 128 * pair : 512 + 128 * pair] = row_sum(heads_back[6 + pair].astype(F32))
     send(M_VG, vgrad, vrecv.at[0], core_dev)
 
     def input_part(quarter):
-        return dims(wide(heads_back, 0, 9, quarter), w_in[...], 1, 1)
+        return sum(
+            dims(beside(heads_back, (pair, 3 + pair, 6 + pair), quarter), w_in[pair], 1, 1)
+            for pair in range(3)
+        )
 
     given(1)
-    for slot in range(2):
+
+    @pl.loop(0, 2)
+    def _(slot):
         give(3, slot, input_part(2 * slot + 1 - b))
+
+    run("t1")
     arrived(M_VG, vrecv.at[0])
     mine = lax.broadcasted_iota(jnp.int32, (16, 768), 0) < 6
     vsend[0] = vgrad[...] + jnp.where(mine, vrecv[0], 0.0)
     send(M_VG + 1, vsend.at[0], vrecv.at[1], x_dev)
-    for i in (2, 1, 3, 0):
-        scatter_near(0, i)
-    for slot in range(2):
+
+    @pl.loop(0, 2)
+    def _(slot):
         own = input_part(2 * slot + b)
         back_rows[slot] = back_rows[slot] + own + take(3, slot)
-    swap_in[0] = back_rows[1 - a].astype(BF16)
-    send(M_GRAD, swap_in.at[0], swap_in.at[1], x_dev)
+
+    cots[0] = back_rows[1 - a].astype(BF16)
+    send(M_GRAD, cots.at[0], cots.at[1], x_dev)
     grad_ref[a] = back_rows[a]
     arrived(M_VG + 1, vrecv.at[1])
     vsend[1] = vsend[0] + vrecv[1]
     send(M_VG + 2, vsend.at[1], vrecv.at[2], y_dev)
-    scatter_end(2)
-    scatter_end(1)
+    run("t2")
     arrived(M_VG + 2, vrecv.at[2])
     vsend[2] = vsend[1] + vrecv[2]
     for j in range(1, 4):
         send(M_VG + 2 + j, vsend.at[2], vrecv.at[2 + j], z_dev(j))
-    for i in (2, 1, 3, 0):
-        scatter_line(0, i)
+    for pack in (3, 4, 2, 0):
+        scatter_end(pack)
+    run("t3")
     every = vsend[2]
     for j in range(1, 4):
         arrived(M_VG + 2 + j, vrecv.at[2 + j])
         every = every + vrecv[2 + j]
-    vout_ref[...] = every
-    arrived(M_GRAD, swap_in.at[1])
-    grad_ref[1 - a] = swap_in[1].astype(F32)
+    vout_ref[...] = pltpu.roll(every, (8 - dp) % 8 * 96, 1)
+    heads_row = every[8:9, :]
+    for kind in range(2):
+        row = heads_row[:, 384 * kind : 384 * kind + 384]
+        low_row = low_lanes((1, 128))
+        third = jnp.where(a == 0, row[:, 256:384], half_turn(row[:, 256:384]))
+        both = jnp.concatenate(
+            (jnp.where(a == 0, row[:, :128], row[:, 128:256]), jnp.where(low_row, third, 0.0)), 1
+        )
+        vout_ref[8 + kind : 9 + kind, 0:256] = pltpu.roll(both, (256 - dp * 24) % 256, 1)
+    vout_ref[6:7, :] = jnp.where(a == 0, vout_ref[6:7, :], vout_ref[7:8, :])
+    arrived(M_GRAD, cots.at[1])
+    grad_ref[1 - a] = cots[1].astype(F32)
     arrived(M_OUT, out_ref.at[1 - a])
-    scatter_end(0)
-
-    for pack in range(3):
+    scatter_end(1)
+
+    for pack in range(5):
         scatter_left(pack)
     given(2)
     given(3)
@@ -1139,7 +1578,7 @@
     left(M_IN, in_ref.at[0])
     left(M_COT, cot_ref.at[0])
     left(M_OUT, swap_out.at[0])
-    left(M_GRAD, swap_in.at[0])
+    left(M_GRAD, cots.at[0])
     for j in range(3):
         left(M_VZ + j, vec_ref)
     left(M_VY, vec_y.at[0])
@@ -1152,27 +1591,68 @@
         left(M_VG + index, vsend.at[0])
 
 
-def layer_call(packs, vectors, masks, tokens, cotangent):
+def finish_kernel(
+    gout_half,
+    gout_wide,
+    vout_ref,
+    query_ref,
+    key_ref,
+    value_ref,
+    project_ref,
+    up_ref,
+    down_ref,
+    query_bias_ref,
+    value_bias_ref,
+    *row_refs
+):
+    first, last = gout_half[0], gout_half[1]
+    query_ref[...] = jnp.concatenate((first[:, 0:128], last[:, 0:64]), 1)
+    key_ref[...] = jnp.concatenate((first[:, 128:256], last[:, 64:128]), 1)
+    value_ref[...] = jnp.concatenate((first[:, 256:384], last[:, 128:192]), 1)
+    gap = jnp.zeros((32, 256), F32)
+    project = jnp.concatenate((last[:, 256:384], last[:, 128:256]), 1)
+    project = jnp.concatenate((project, gap), 0).T
+    project_ref[0:128, :] = project[0:128, :96]
+    project_ref[128:192, :] = project[192:256, :96]
+    up_ref[...] = gout_wide[0]
+    down_ref[...] = jnp.concatenate((gout_half[2], gout_half[3]), 1)
+    query_bias_ref[...] = vout_ref[8, 0:24]
+    value_bias_ref[...] = vout_ref[9, 0:24]
+    for row, ref in enumerate(row_refs):
+        ref[...] = vout_ref[row, 0:96]
+
+
+def layer_call(weights, rows, biases, random_blocks, tokens, cotangent):
     vmem = pltpu.VMEM
     anywhere = pl.BlockSpec(memory_space=pltpu.VMEM)
     shape = jax.ShapeDtypeStruct
+    def both(*dims_, kind=BF16):
+        return (vmem((4,) + dims_ + (384,), kind), vmem((1,) + dims_ + (768,), kind))
+
     scratch = [
-        vmem((2, 3, 768, 768), BF16),
+        vmem((2, 96, 384), BF16),
+        vmem((16, 768), BF16),
+        vmem((48, 128), BF16),
+        vmem((2, 2, 768, 384), BF16),
+        vmem((2, 2, 768, 768), BF16),
         vmem((3, 16, 768), BF16),
         vmem((2, 16, 768), BF16),
         vmem((2, 16, 768), BF16),
-        vmem((2, 96, 128), BF16),
+        vmem((2, 48, 128), BF16),
         vmem((4, TILE, 768), BF16),
+        vmem((768, 4 * TILE), BF16),
         vmem((2, TILE, 768), BF16),
-        vmem((768, 1152), BF16),
+        vmem((3, 768, 384), BF16),
         vmem((768, 384), BF16),
         vmem((3, 2, 4, 4, 1024), F32),
         vmem((3, 2, 16, 1024), F32),
         vmem((9, 1024, 128), BF16),
+        vmem((3, 128, 1024), BF16),
         vmem((3, 1024, 128), BF16),
-        vmem((3, 1024, 128), F32),
-        vmem((16, 1024), F32),
+        vmem((3, 2, 1, 1024), F32),
+        vmem((8, 1024), F32),
         vmem((4, TILE, 768), BF16),
+        vmem((768, 4 * TILE), BF16),
         vmem((4, TILE, 768), BF16),
         vmem((4, TILE, 768), BF16),
         vmem((2, TILE, 768), F32),
@@ -1182,19 +1662,19 @@
         vmem((2, 4, TILE, 768), BF16),
         vmem((TILE, 768), F32),
         vmem((2, 2, TILE, 768), BF16),
-        vmem((4, 2, TILE, 768), BF16),
+        vmem((2, 2, TILE, 768), BF16),
         vmem((3, 1024, 128), BF16),
         vmem((1024, 128), F32),
         vmem((1024, 128), F32),
         vmem((9, 1024, 128), BF16),
-        vmem((8, 128), F32),
-        vmem((3, 4, 48, 768), BF16),
-        vmem((3, 4, 48, 768), BF16),
-        vmem((3, 4, 96, 768), BF16),
-        vmem((3, 4, 96, 768), BF16),
-        vmem((3, 3, 96, 768), BF16),
-        vmem((3, 96, 768), F32),
-        vmem((2, TILE, 768), BF16),
+        vmem((768, 384), BF16),
+        both(4, 48),
+        both(4, 48),
+        both(4, 96),
+        both(4, 96),
+        both(3, 96 - LEAN),
+        both(3, 4, LEAN),
+        both(96, kind=F32),
         vmem((2, TILE, 768), BF16),
         vmem((16, 768), F32),
         vmem((3, 16, 768), F32),
@@ -1207,16 +1687,17 @@
         out_shape=(
             shape(tokens.shape, BF16),
             shape(tokens.shape, F32),
-            shape(packs.shape, F32),
-            shape(vectors.shape, F32),
+            shape((4, 96, 384), F32),
+            shape((1, 96, 768), F32),
+            shape((16, 768), F32),
         ),
-        in_specs=[anywhere] * 5,
-        out_specs=(anywhere,) * 4,
+        in_specs=[anywhere] * 6 + [(anywhere,) * 7] + [anywhere] * 5,
+        out_specs=(anywhere,) * 5,
         scratch_shapes=scratch,
         compiler_params=pltpu.CompilerParams(
-            collective_id=0, has_side_effects=True, vmem_limit_bytes=62 << 20
+            collective_id=0, has_side_effects=True, vmem_limit_bytes=63 << 20
         ),
-    )(packs, vectors, masks, tokens, cotangent)
+    )(*weights, rows, *biases, random_blocks, tokens, cotangent)
 
 
 def local_fast(
@@ -1239,78 +1720,47 @@
     second_shift,
     cotangent,
 ):
-    dp, tensor = lax.axis_index("dp"), lax.axis_index("tensor")
-    out_turned = out_weight.T
-    first_pack = jnp.concatenate(
-        (
-            query_weight[:, :128],
-            key_weight[:, :128],
-            value_weight[:, :128],
-            query_weight[:, 128:],
-            key_weight[:, 128:],
-            value_weight[:, 128:],
-            out_turned[:, 128:],
-            out_turned[:, :128],
-        ),
-        1,
-    )
-    packs = jnp.stack((first_pack, up_weight, down_weight.T))
-
-    def placed(values):
-        width = values.shape[0]
-        spots = jnp.arange(8 * width, dtype=jnp.int32) // width
-        return jnp.where(spots == dp, jnp.tile(values, 8), jnp.zeros((), values.dtype))
-
-    query_row, value_row = placed(query_bias), placed(value_bias)
-    gap = jnp.zeros((128,), BF16)
-    in_row = jnp.concatenate(
-        (query_row[:128], gap, value_row[:128], query_row[128:], gap[:64], value_row[128:], gap, gap[:64])
-    )
-    rows = [
-        placed(v) for v in (out_bias, first_gain, first_shift, down_bias, second_gain, second_shift, up_bias)
-    ]
-    vectors = jnp.concatenate((jnp.stack(rows + [in_row]), jnp.zeros((8, 768), BF16)))
-    allowed = block_allowed(random_blocks, random_blocks.shape[1]).astype(BF16)
-    masks = jnp.concatenate((allowed.reshape(48, 16), allowed.transpose(0, 2, 1).reshape(48, 16)))
-    masks = jnp.pad(masks, ((0, 0), (0, 112)))
-    output, input_grad, grads, sums = layer_call(packs, vectors, masks, inputs, cotangent)
-    first = grads[0]
-    query_grad = jnp.concatenate((first[:, 0:128], first[:, 384:448]), 1)
-    key_grad = jnp.concatenate((first[:, 128:256], first[:, 448:512]), 1)
-    value_grad = jnp.concatenate((first[:, 256:384], first[:, 512:576]), 1)
-    out_grad = jnp.concatenate((first[:, 640:768], first[:, 576:640]), 1).T
-    side = tensor // 2
-
-    def own(row):
-        return lax.dynamic_slice(row, (dp * 96,), (96,))
-
-    def head_bias(row):
-        both = jnp.concatenate(
-            (
-                lax.dynamic_slice(row, (side * 128,), (128,)),
-                lax.dynamic_slice(row, (256 + side * 64,), (64,)),
-            )
-        )
-        return lax.dynamic_slice(both, (dp * 24,), (24,))
-
+    output, input_grad, half_grads, wide_grads, sums = layer_call(
+        (query_weight, key_weight, value_weight, down_weight.T, up_weight, out_weight),
+        (out_bias, first_gain, first_shift, down_bias, second_gain, second_shift, up_bias),
+        (query_bias, value_bias),
+        random_blocks.transpose(0, 2, 1),
+        inputs,
+        cotangent,
+    )
+    like = lambda array: jax.ShapeDtypeStruct(array.shape, F32)
+    whole = pl.BlockSpec(memory_space=pltpu.VMEM)
+    outs = (query_weight, key_weight, value_weight, out_weight, up_weight, up_weight)
+    outs += (query_bias, value_bias)
+    outs += (second_gain, second_shift, down_bias, first_gain, first_shift, out_bias, up_bias)
+    done = pl.pallas_call(
+        finish_kernel,
+        out_shape=tuple(like(array) for array in outs),
+        in_specs=[whole] * 3,
+        out_specs=(whole,) * len(outs),
+    )(half_grads, wide_grads, sums)
+    query_grad, key_grad, value_grad, out_grad, up_grad, down_grad = done[:6]
+    query_bias_grad, value_bias_grad = done[6:8]
+    second_gain_grad, second_shift_grad, down_bias_grad = done[8:11]
+    first_gain_grad, first_shift_grad, out_bias_grad, up_bias_grad = done[11:]
     return (
         output,
         input_grad,
         query_grad,
-        head_bias(sums[8, :384]),
+        query_bias_grad,
         key_grad,
         value_grad,
-        head_bias(sums[8, 384:]),
+        value_bias_grad,
         out_grad,
-        own(sums[5]),
-        own(sums[3]),
-        own(sums[4]),
-        grads[1],
-        own(lax.dynamic_slice(sums, (6 + side, 0), (1, 768))[0]),
-        grads[2].T,
-        own(sums[2]),
-        own(sums[0]),
-        own(sums[1]),
+        out_bias_grad,
+        first_gain_grad,
+        first_shift_grad,
+        up_grad,
+        up_bias_grad,
+        down_grad.T,
+        down_bias_grad,
+        second_gain_grad,
+        second_shift_grad,
     )
 
 

time: 210 us -> 172 us (0.82)
  local copies, waits for them, and re-layouts: 20.8 us -> 3.21 us
  Pallas kernels: 182 us -> 168 us
  other arithmetic: 4.75 us -> 0 us
    pallas_call x1, Pallas kernels: 182 us -> 166 us  [layer_call(): pl.pallas_call(layer_kernel, out_shape=(shape(tokens.shape, BF16), shape(...]
    slice x14 -> x0, local copies, waits for them, and re-layouts: 6.31 us -> none  [the longest x1 0.97 us: local_fast(): sums[1]]
    dynamic_slice x13 -> x0, local copies, waits for them, and re-layouts: 6.09 us -> none  [the longest x7 4.77 us: own(): return lax.dynamic_slice(row, (dp * 96,), (96,))]
    pallas_call x0 -> x1, Pallas kernels: none -> 2.35 us  [local_fast(): pl.pallas_call(finish_kernel, out_shape=tuple((like(array) for array in o...]
where the time goes in v2:
time: 172 us
  Pallas kernels  168 us (98%)
  local copies, waits for them, and re-layouts  3.21 us (2%)
    pallas_call x1, Pallas kernels, layer_call(): pl.pallas_call(layer_kernel, out_shape=(shape(tokens.shape, BF16), shape(...  166 us

profile of v2, /device:TPU:0, one launch (start us, length us, event | category | flops | bytes accessed | tf_op | source)
XLA Modules:
  0.0 172.1 jit_solution(14352966445150047582)
XLA Ops:
  0.7 165.8 %shard_map.305 = (bf16[2,256,768]{2,1,0:T(8,128)(2,1)}, f32[2,256,768]{2,1,0:T(8,128)}, f32[4,96,384]{2,1,0:T(8,128)}, f32[1,96,768]{2,1,0:T(8,128)}, f32[16,768]{1,0:T(8,128)}) custom-call(bf16[96,192]{1,0:T(8,128)(2,1)} %query_ref.1, bf16[96,192]{1,0:T(8,128)(2,1)} %key_ref.1, bf16[96,192]{1,0:T(8,128)(2,1)} %value_ref.1, bf16[96,768]{1,0:T(8,128)(2,1)} %bitcast.3, ...), custom_call_target="tpu_custom_call" | custom-call | tf_op jit(solution)/shard_map/pallas_call | solution.py:1685
  166.5 0.0 copy-start
  166.5 2.3 %shard_map.306 = (f32[96,192]{1,0:T(8,128)}, f32[96,192]{1,0:T(8,128)}, f32[96,192]{1,0:T(8,128)}, f32[192,96]{1,0:T(8,128)}, f32[96,768]{1,0:T(8,128)}, /*index...) custom-call(f32[4,96,384]{2,1,0:T(8,128)} %get-tuple-element.39.gout, ...), custom_call_target="tpu_custom_call" | custom-call | tf_op jit(solution)/shard_map/pallas_call | solution.py:1736
  168.9 2.1 %copy.37 = bf16[2,256,768]{2,1,0:T(8,128)(2,1)} copy(bf16[2,256,768]{2,1,0:T(8,128)(2,1)} %get-tuple-element.74) | data formatting | bytes 1572864
  170.9 0.0 copy-done
  170.9 1.1 copy.38
Async XLA Ops:
  166.5 4.4 %copy-start = (f32[2,256,768]{2,1,0:T(8,128)S(1)}, f32[2,256,768]{2,1,0:T(8,128)}, u32[]{:S(2)}) copy-start(f32[2,256,768]{2,1,0:T(8,128)} %get-tuple-element.75) | copy-start | bytes 4718596

commit v3 on v2

--- a/solution.py
+++ b/solution.py
@@ -724,6 +724,23 @@
 
 
 def layer_kernel(
+    query_far,
+    key_far,
+    value_far,
+    down_far,
+    up_far,
+    project_far,
+    rows_far,
+    query_bias_far,
+    value_bias_far,
+    picks_far,
+    in_far,
+    cot_far,
+    out_ref,
+    grad_ref,
+    gout_half,
+    gout_wide,
+    vout_ref,
     query_ref,
     key_ref,
     value_ref,
@@ -736,11 +753,6 @@
     picks_ref,
     in_ref,
     cot_ref,
-    out_ref,
-    grad_ref,
-    gout_half,
-    gout_wide,
-    vout_ref,
     pack_ref,
     vec_ref,
     mask_ref,
@@ -792,6 +804,7 @@
     vrecv,
     send_sem,
     recv_sem,
+    local_sem,
 ):
     dp, tensor = lax.axis_index("dp"), lax.axis_index("tensor")
     z, y = dp // 2, dp % 2
@@ -809,6 +822,32 @@
     barrier = pltpu.get_barrier_semaphore()
     for dev in (core_dev, x_dev, y_dev, z_dev(1), z_dev(2), z_dev(3)):
         pl.semaphore_signal(barrier, inc=1, device_id=dev, device_id_type=MESH)
+    loads = [
+        (query_far, query_ref),
+        (key_far, key_ref),
+        (value_far, value_ref),
+        (in_far, in_ref),
+        (project_far, project_ref),
+        (picks_far, picks_ref),
+        (query_bias_far, query_bias_ref),
+        (value_bias_far, value_bias_ref),
+        *zip(rows_far, row_refs),
+        (up_far, up_ref),
+        (down_far, down_ref),
+        (cot_far, cot_ref),
+    ]
+    loads = [
+        pltpu.make_async_copy(src, goal, local_sem.at[index])
+        for index, (src, goal) in enumerate(loads)
+    ]
+    for load in loads:
+        load.start()
+
+    def store_far(index, src, goal):
+        return pltpu.make_async_copy(src, goal, local_sem.at[index])
+
+    for load in loads:
+        load.wait()
     pl.semaphore_wait(barrier, 6)
 
     def copy(index, src, dst, dev):
@@ -1335,7 +1374,7 @@
         vgrad[1:2, :] += row_sum(upstream)
         vgrad[2:3, :] += row_sum(back)
 
-    out_ref[a] = swap_out[a]
+    store_far(20, swap_out.at[a], out_ref.at[a]).start()
     send(M_OUT, swap_out.at[1 - a], out_ref.at[a], x_dev)
     for pack in range(4):
         gather_left(pack)
@@ -1538,7 +1577,7 @@
 
     cots[0] = back_rows[1 - a].astype(BF16)
     send(M_GRAD, cots.at[0], cots.at[1], x_dev)
-    grad_ref[a] = back_rows[a]
+    store_far(21, back_rows.at[a], grad_ref.at[a]).start()
     arrived(M_VG + 1, vrecv.at[1])
     vsend[1] = vsend[0] + vrecv[1]
     send(M_VG + 2, vsend.at[1], vrecv.at[2], y_dev)
@@ -1566,9 +1605,14 @@
         vout_ref[8 + kind : 9 + kind, 0:256] = pltpu.roll(both, (256 - dp * 24) % 256, 1)
     vout_ref[6:7, :] = jnp.where(a == 0, vout_ref[6:7, :], vout_ref[7:8, :])
     arrived(M_GRAD, cots.at[1])
-    grad_ref[1 - a] = cots[1].astype(F32)
+    hat_first[0] = cots[1].astype(F32)
+    store_far(22, hat_first.at[0], grad_ref.at[1 - a]).start()
     arrived(M_OUT, out_ref.at[1 - a])
     scatter_end(1)
+
+    store_far(20, swap_out.at[a], out_ref.at[a]).wait()
+    store_far(21, back_rows.at[a], grad_ref.at[a]).wait()
+    store_far(22, hat_first.at[0], grad_ref.at[1 - a]).wait()
 
     for pack in range(5):
         scatter_left(pack)
@@ -1595,6 +1639,8 @@
     gout_half,
     gout_wide,
     vout_ref,
+    from_output,
+    from_grad,
     query_ref,
     key_ref,
     value_ref,
@@ -1603,8 +1649,27 @@
     down_ref,
     query_bias_ref,
     value_bias_ref,
-    *row_refs
+    second_gain_ref,
+    second_shift_ref,
+    down_bias_ref,
+    first_gain_ref,
+    first_shift_ref,
+    out_bias_ref,
+    up_bias_ref,
+    to_output,
+    to_grad,
 ):
+    row_refs = (
+        second_gain_ref,
+        second_shift_ref,
+        down_bias_ref,
+        first_gain_ref,
+        first_shift_ref,
+        out_bias_ref,
+        up_bias_ref,
+    )
+    to_output[...] = from_output[...]
+    to_grad[...] = from_grad[...]
     first, last = gout_half[0], gout_half[1]
     query_ref[...] = jnp.concatenate((first[:, 0:128], last[:, 0:64]), 1)
     key_ref[...] = jnp.concatenate((first[:, 128:256], last[:, 64:128]), 1)
@@ -1625,11 +1690,16 @@
 def layer_call(weights, rows, biases, random_blocks, tokens, cotangent):
     vmem = pltpu.VMEM
     anywhere = pl.BlockSpec(memory_space=pltpu.VMEM)
+    far = pl.BlockSpec(memory_space=pl.ANY)
     shape = jax.ShapeDtypeStruct
     def both(*dims_, kind=BF16):
         return (vmem((4,) + dims_ + (384,), kind), vmem((1,) + dims_ + (768,), kind))
 
+    like = lambda array: vmem(array.shape, array.dtype)
     scratch = [
+        *(like(array) for array in weights),
+        tuple(like(array) for array in rows),
+        *(like(array) for array in (*biases, random_blocks, tokens, cotangent)),
         vmem((2, 96, 384), BF16),
         vmem((16, 768), BF16),
         vmem((48, 128), BF16),
@@ -1681,6 +1751,7 @@
         vmem((6, 16, 768), F32),
         pltpu.SemaphoreType.DMA((MESSAGES,)),
         pltpu.SemaphoreType.DMA((MESSAGES,)),
+        pltpu.SemaphoreType.DMA((24,)),
     ]
     return pl.pallas_call(
         layer_kernel,
@@ -1691,8 +1762,8 @@
             shape((1, 96, 768), F32),
             shape((16, 768), F32),
         ),
-        in_specs=[anywhere] * 6 + [(anywhere,) * 7] + [anywhere] * 5,
-        out_specs=(anywhere,) * 5,
+        in_specs=[far] * 6 + [(far,) * 7] + [far] * 5,
+        out_specs=(far,) * 2 + (anywhere,) * 3,
         scratch_shapes=scratch,
         compiler_params=pltpu.CompilerParams(
             collective_id=0, has_side_effects=True, vmem_limit_bytes=63 << 20
@@ -1735,14 +1806,16 @@
     outs += (second_gain, second_shift, down_bias, first_gain, first_shift, out_bias, up_bias)
     done = pl.pallas_call(
         finish_kernel,
-        out_shape=tuple(like(array) for array in outs),
-        in_specs=[whole] * 3,
-        out_specs=(whole,) * len(outs),
-    )(half_grads, wide_grads, sums)
+        out_shape=tuple(like(array) for array in outs)
+        + tuple(jax.ShapeDtypeStruct(array.shape, array.dtype) for array in (output, input_grad)),
+        in_specs=[whole] * 5,
+        out_specs=(whole,) * (len(outs) + 2),
+    )(half_grads, wide_grads, sums, output, input_grad)
     query_grad, key_grad, value_grad, out_grad, up_grad, down_grad = done[:6]
     query_bias_grad, value_bias_grad = done[6:8]
     second_gain_grad, second_shift_grad, down_bias_grad = done[8:11]
-    first_gain_grad, first_shift_grad, out_bias_grad, up_bias_grad = done[11:]
+    first_gain_grad, first_shift_grad, out_bias_grad, up_bias_grad = done[11:15]
+    output, input_grad = done[15:]
     return (
         output,
         input_grad,

time: 172 us -> 169 us (0.983)
  local copies, waits for them, and re-layouts: 3.21 us -> 0 us
    unnamed x4 -> x0, local copies, waits for them, and re-layouts: 3.21 us -> none
where the time goes in v3:
time: 169 us
  Pallas kernels  168 us (99%)
    pallas_call x1, Pallas kernels, layer_call(): pl.pallas_call(layer_kernel, out_shape=(shape(tokens.shape, BF16), shape(...  164 us
    pallas_call x1, Pallas kernels, local_fast(): pl.pallas_call(finish_kernel, out_shape=tuple((like(array) for array in o...  3.78 us

profile of v3, /device:TPU:0, one launch (start us, length us, event | category | flops | bytes accessed | tf_op | source)
XLA Modules:
  0.0 168.8 jit_solution(5367065332091075271)
XLA Ops:
  0.7 164.3 %shard_map.305 = (bf16[2,256,768]{2,1,0:T(8,128)(2,1)}, f32[2,256,768]{2,1,0:T(8,128)}, f32[4,96,384]{2,1,0:T(8,128)}, f32[1,96,768]{2,1,0:T(8,128)}, f32[16,768]{1,0:T(8,128)}) custom-call(bf16[96,192]{1,0:T(8,128)(2,1)} %query_far.1, bf16[96,192]{1,0:T(8,128)(2,1)} %key_far.1, bf16[96,192]{1,0:T(8,128)(2,1)} %value_far.1, bf16[96,768]{1,0:T(8,128)(2,1)} %bitcast.3, ...), custom_call_target="tpu_custom_call" | custom-call | tf_op jit(solution)/shard_map/pallas_call | solution.py:1756
  165.0 3.8 %shard_map.306 = (f32[96,192]{1,0:T(8,128)}, f32[96,192]{1,0:T(8,128)}, f32[96,192]{1,0:T(8,128)}, f32[192,96]{1,0:T(8,128)}, f32[96,768]{1,0:T(8,128)}, /*index...) custom-call(f32[4,96,384]{2,1,0:T(8,128)} %get-tuple-element.39.gout, ...), custom_call_target="tpu_custom_call" | custom-call | tf_op jit(solution)/shard_map/pallas_call | solution.py:1807

commit v4 on v3

--- a/solution.py
+++ b/solution.py
@@ -848,7 +848,6 @@
 
     for load in loads:
         load.wait()
-    pl.semaphore_wait(barrier, 6)
 
     def copy(index, src, dst, dev):
         return pltpu.make_async_remote_copy(
@@ -1154,6 +1153,7 @@
             picks = jnp.concatenate((picks, jnp.full((1, 112), -1, jnp.int32)), 1)
             allowed = allowed | (picks == row)
         mask_ref[16 * head : 16 * head + 16, :] = jnp.where(allowed, 1.0, 0.0).astype(BF16)
+    pl.semaphore_wait(barrier, 6)
     send(M_MASK, mask_ref, masks.at[a], x_dev)
     send(M_IN, in_ref.at[1 - a], tokens.at[tensor], x_dev)
     for j in range(1, 4):

time: 169 us -> 168 us (level)
  no operation moved by 1% of the time
where the time goes in v4:
time: 168 us
  Pallas kernels  167 us (99%)
    pallas_call x1, Pallas kernels, layer_call(): pl.pallas_call(layer_kernel, out_shape=(shape(tokens.shape, BF16), shape(...  164 us
    pallas_call x1, Pallas kernels, local_fast(): pl.pallas_call(finish_kernel, out_shape=tuple((like(array) for array in o...  3.78 us

profile of v4, /device:TPU:0, one launch (start us, length us, event | category | flops | bytes accessed | tf_op | source)
XLA Modules:
  0.0 168.0 jit_solution(1084138094035451953)
XLA Ops:
  0.7 163.5 %shard_map.305 = (bf16[2,256,768]{2,1,0:T(8,128)(2,1)}, f32[2,256,768]{2,1,0:T(8,128)}, f32[4,96,384]{2,1,0:T(8,128)}, f32[1,96,768]{2,1,0:T(8,128)}, f32[16,768]{1,0:T(8,128)}) custom-call(bf16[96,192]{1,0:T(8,128)(2,1)} %query_far.1, bf16[96,192]{1,0:T(8,128)(2,1)} %key_far.1, bf16[96,192]{1,0:T(8,128)(2,1)} %value_far.1, bf16[96,768]{1,0:T(8,128)(2,1)} %bitcast.3, ...), custom_call_target="tpu_custom_call" | custom-call | tf_op jit(solution)/shard_map/pallas_call | solution.py:1756
  164.2 3.8 %shard_map.306 = (f32[96,192]{1,0:T(8,128)}, f32[96,192]{1,0:T(8,128)}, f32[96,192]{1,0:T(8,128)}, f32[192,96]{1,0:T(8,128)}, f32[96,768]{1,0:T(8,128)}, /*index...) custom-call(f32[4,96,384]{2,1,0:T(8,128)} %get-tuple-element.39.gout, ...), custom_call_target="tpu_custom_call" | custom-call | tf_op jit(solution)/shard_map/pallas_call | solution.py:1807

commit v5 on v4

--- a/solution.py
+++ b/solution.py
@@ -1351,14 +1351,14 @@
         run("u" + str(2 + slot))
     gather_end(3)
 
-    @pl.loop(0, 2)
+    @pl.loop(0, 2, unroll=True)
     def _(slot):
         give(1, slot, feed_down(2 * slot + 1 - b))
 
     arrived(M_COT, cots.at[1 - a])
     vgrad[...] = jnp.zeros_like(vgrad)
 
-    @pl.loop(0, 2)
+    @pl.loop(0, 2, unroll=True)
     def _(slot):
         quarter = 2 * slot + b
         own = feed_down(quarter)

time: 168 us -> 168 us (level)
  no operation moved by 1% of the time
where the time goes in v5:
time: 168 us
  Pallas kernels  167 us (99%)
    pallas_call x1, Pallas kernels, layer_call(): pl.pallas_call(layer_kernel, out_shape=(shape(tokens.shape, BF16), shape(...  163 us
    pallas_call x1, Pallas kernels, local_fast(): pl.pallas_call(finish_kernel, out_shape=tuple((like(array) for array in o...  3.78 us

profile of v5, /device:TPU:0, one launch (start us, length us, event | category | flops | bytes accessed | tf_op | source)
XLA Modules:
  0.0 167.9 jit_solution(15056721879137000000)
XLA Ops:
  0.7 163.4 %shard_map.305 = (bf16[2,256,768]{2,1,0:T(8,128)(2,1)}, f32[2,256,768]{2,1,0:T(8,128)}, f32[4,96,384]{2,1,0:T(8,128)}, f32[1,96,768]{2,1,0:T(8,128)}, f32[16,768]{1,0:T(8,128)}) custom-call(bf16[96,192]{1,0:T(8,128)(2,1)} %query_far.1, bf16[96,192]{1,0:T(8,128)(2,1)} %key_far.1, bf16[96,192]{1,0:T(8,128)(2,1)} %value_far.1, bf16[96,768]{1,0:T(8,128)(2,1)} %bitcast.3, ...), custom_call_target="tpu_custom_call" | custom-call | tf_op jit(solution)/shard_map/pallas_call | solution.py:1756
  164.1 3.8 %shard_map.306 = (f32[96,192]{1,0:T(8,128)}, f32[96,192]{1,0:T(8,128)}, f32[96,192]{1,0:T(8,128)}, f32[192,96]{1,0:T(8,128)}, f32[96,768]{1,0:T(8,128)}, /*index...) custom-call(f32[4,96,384]{2,1,0:T(8,128)} %get-tuple-element.39.gout, ...), custom_call_target="tpu_custom_call" | custom-call | tf_op jit(solution)/shard_map/pallas_call | solution.py:1807
